TPU v7x, 128 devices: a whole 4x4x4 slice. The times are simulated.
128 devices in a mesh: dp: 16 (over x, y), expert: 8 (over z, core).
Axes of the slice: x: 4, y: 4, z: 4, core: 2. Of those that a mesh axis runs over, the one named last changes fastest.
Arguments:
- layer_input: bfloat16 [16384, 2560], P(('dp', 'expert')), may hold values from -6 to 6
- output_grad: bfloat16 [16384, 2560], P(('dp', 'expert')), may hold values from -6 to 6
- expert_ids: int32 [16384, 2], P(('dp', 'expert')), may hold values from 0 to 7, all different within a row; in each aligned block of 128 rows (0 to 127, 128 to 255, ...) at most 48 rows name the same one
- gate_probs: bfloat16 [16384, 2], P(('dp', 'expert')), may hold values from 0.099609375 to 0.59765625
- gate_weight: float32 [8, 2560, 1536], P('expert', 'dp'), may hold values from -0.125 to 0.125
- up_weight: float32 [8, 2560, 1536], P('expert', 'dp'), may hold values from -0.125 to 0.125
- down_weight: float32 [8, 1536, 2560], P('expert', 'dp'), may hold values from -0.15625 to 0.15625
- gate_moment: float32 [8, 2560, 1536], P('expert', 'dp'), may hold values from -12 to 12
- up_moment: float32 [8, 2560, 1536], P('expert', 'dp'), may hold values from -12 to 12
- down_moment: float32 [8, 1536, 2560], P('expert', 'dp'), may hold values from -12 to 12
- gate_second: float32 [8, 2560, 1536], P('expert', 'dp'), may hold values from 1 to 100
- up_second: float32 [8, 2560, 1536], P('expert', 'dp'), may hold values from 1 to 100
- down_second: float32 [8, 1536, 2560], P('expert', 'dp'), may hold values from 1 to 100
Outputs:
- input_grad: bfloat16 [16384, 2560], P(('dp', 'expert'))
- prob_grad: bfloat16 [16384, 2], P(('dp', 'expert'))
- new_gate_weight: float32 [8, 2560, 1536], P('expert', 'dp')
- new_up_weight: float32 [8, 2560, 1536], P('expert', 'dp')
- new_down_weight: float32 [8, 1536, 2560], P('expert', 'dp')
- new_gate_moment: float32 [8, 2560, 1536], P('expert', 'dp')
- new_up_moment: float32 [8, 2560, 1536], P('expert', 'dp')
- new_down_moment: float32 [8, 1536, 2560], P('expert', 'dp')
- new_gate_second: float32 [8, 2560, 1536], P('expert', 'dp')
- new_up_second: float32 [8, 2560, 1536], P('expert', 'dp')
- new_down_second: float32 [8, 1536, 2560], P('expert', 'dp')
Inputs may be any that keep to these rules, and one draw needn't show every extreme that they name: `expert_ids`: each token names 2 different experts. Among the (token, pick) pairs of one device's 128 tokens, no expert is named more than 48 times, and in every draw some device's tokens name some expert exactly 48 times.
All inputs are finite; a program needn't handle non-finite values.
Results may differ from a plain program's by a relative error of at most 0.025.
Values may be sent and summed in bfloat16 or wider, within the bound.
No kernel may reach another device: no remote copies, remote signals or barrier semaphores. Data moves between devices by JAX's collectives and lax.ppermute only.
A program may use at most 256 MiB of HBM per device.

v0:
```python
import jax
import jax.numpy as jnp
from jax import lax
from jax.experimental import pallas as pl
from jax.experimental.pallas import tpu as pltpu
from jax.sharding import Mesh
from jax.sharding import PartitionSpec as P

beta_one = 0.9
beta_two = 0.95
learn_rate = 0.003
decay_rate = 0.1
epsilon = 1e-08
correct_one = 1.0 - 2.6561398887587e-05
correct_two = 1.0 - 0.005920529220333

LANES = 128
GROUPS = 8
f32 = jnp.float32
bf16 = jnp.bfloat16

PLUS = [(i, (i + 1) % 4) for i in range(4)]
MINUS = [(i, (i - 1) % 4) for i in range(4)]
SWAP = [(0, 1), (1, 0)]
PAIR_A = [(2 * yl + c, 2 * c + yl) for yl in range(2) for c in range(2)]
PAIR_B = [(2 * yl + c, 2 * c + 1 - yl) for yl in range(2) for c in range(2)]


def _cycle():
    pairs = []
    for x1 in range(2):
        for x0 in range(2):
            for yh in range(2):
                for yl in range(2):
                    for c in range(2):
                        src = (((x1 * 2 + x0) * 2 + yh) * 2 + yl) * 2 + c
                        dst = (((x1 * 2 + yh) * 2 + yl) * 2 + c) * 2 + x0
                        pairs.append((src, dst))
    return pairs


CYCLE = _cycle()
CYCLE_AXES = ("x", "yh", "yl", "c")


def back(pairs):
    return [(d, s) for s, d in pairs]


join = lax.optimization_barrier


def adamw(weight, moment, second, grad):
    moment_new = beta_one * moment + (1.0 - beta_one) * grad
    second_new = beta_two * second + (1.0 - beta_two) * grad * grad
    update = moment_new / correct_one / (jnp.sqrt(second_new / correct_two) + epsilon)
    return (weight - learn_rate * (update + decay_rate * weight), moment_new, second_new)


def one_hots(ids, capacity):
    tok = ids.shape[1]
    experts = lax.broadcasted_iota(jnp.int32, (GROUPS, tok), 0)
    named = [(experts == ids[k : k + 1, :]).astype(f32) for k in range(2)]
    earlier = (
        lax.broadcasted_iota(jnp.int32, (tok, tok), 0)
        < lax.broadcasted_iota(jnp.int32, (tok, tok), 1)
    ).astype(f32)
    count = jnp.dot(
        (named[0] + named[1]).astype(bf16), earlier.astype(bf16), preferred_element_type=f32
    )
    slot = lax.broadcasted_iota(jnp.int32, (GROUPS * capacity, tok), 0)
    hots = []
    for k in range(2):
        rank = jnp.sum(named[k] * count, axis=0, keepdims=True).astype(jnp.int32)
        expert = ids[k : k + 1, :]
        dest = ((expert & 1) * 4 + (expert >> 1)) * capacity + rank
        hots.append((slot == dest).astype(f32))
    return hots


def block_of(width):
    return 512 if width % 512 == 0 else width


def pack_kernel(capacity, width, ids_ref, probs_ref, x_ref, y_ref, out_ref):
    first, second = one_hots(ids_ref[...], capacity)
    hot = (first + second).astype(bf16)
    probs = probs_ref[...]
    gates = (first * probs[0:1, :] + second * probs[1:2, :]).astype(bf16)
    ones = jnp.ones((gates.shape[1], LANES), bf16)
    out_ref[:, 2 * width :] = jnp.dot(gates, ones, preferred_element_type=f32).astype(bf16)
    block = block_of(width)

    def step(i, carry):
        at = pl.multiple_of(i * block, block)
        cols = pl.ds(at, block)
        out_ref[:, cols] = jnp.dot(
            hot, x_ref[:, cols], preferred_element_type=f32
        ).astype(bf16)
        out_ref[:, pl.ds(pl.multiple_of(at + width, block), block)] = jnp.dot(
            hot, y_ref[:, cols], preferred_element_type=f32
        ).astype(bf16)
        return carry

    lax.fori_loop(0, width // block, step, 0)


def unpack_kernel(capacity, width, ids_ref, rows_ref, x_ref, prob_ref):
    first, second = one_hots(ids_ref[...], capacity)
    hot = (first + second).astype(bf16)
    block = block_of(width)

    def step(i, carry):
        cols = pl.ds(pl.multiple_of(i * block, block), block)
        x_ref[:, cols] = lax.dot_general(
            hot, rows_ref[:, cols], (((0,), (0,)), ((), ())), preferred_element_type=f32
        ).astype(bf16)
        return carry

    lax.fori_loop(0, width // block, step, 0)
    q_col = rows_ref[:, width:].astype(f32)
    prob_ref[0:1, :] = jnp.sum(first * q_col, axis=0, keepdims=True).astype(bf16)
    prob_ref[1:2, :] = jnp.sum(second * q_col, axis=0, keepdims=True).astype(bf16)


def vmem_specs(count):
    return [pl.BlockSpec(memory_space=pltpu.VMEM) for _ in range(count)]


def pack_rows(ids, probs, x, y, capacity):
    width = x.shape[1]
    return pl.pallas_call(
        lambda *refs: pack_kernel(capacity, width, *refs),
        out_shape=jax.ShapeDtypeStruct((GROUPS * capacity, 2 * width + LANES), bf16),
        in_specs=vmem_specs(4),
        out_specs=vmem_specs(1)[0],
        compiler_params=pltpu.CompilerParams(vmem_limit_bytes=40 << 20),
        name="pack_rows",
    )(ids, probs, x, y)


def unpack_rows(ids, rows, width, capacity):
    tok = ids.shape[1]
    return pl.pallas_call(
        lambda *refs: unpack_kernel(capacity, width, *refs),
        out_shape=(
            jax.ShapeDtypeStruct((tok, width), bf16),
            jax.ShapeDtypeStruct((2, tok), bf16),
        ),
        in_specs=vmem_specs(2),
        out_specs=tuple(vmem_specs(2)),
        compiler_params=pltpu.CompilerParams(vmem_limit_bytes=40 << 20),
        name="unpack_rows",
    )(ids, rows)


def term_kernel(x_ref, gate_ref, up_ref, gate_out, up_out):
    for d_ref, out in ((gate_ref, gate_out), (up_ref, up_out)):
        out[...] = lax.dot_general(
            x_ref[...], d_ref[...], (((0,), (0,)), ((), ())), preferred_element_type=f32
        ).astype(bf16)


SMALL = pl.CostEstimate(flops=1, transcendentals=0, bytes_accessed=1)


def x_terms(x_rows, gate_grad, up_grad):
    count, width = x_rows.shape
    n = gate_grad.shape[1]
    block = block_of(width)
    out = jax.ShapeDtypeStruct((width, n), bf16)
    whole = pl.BlockSpec((count, n), lambda i: (0, 0))
    part = pl.BlockSpec((block, n), lambda i: (i, 0))
    return pl.pallas_call(
        term_kernel,
        out_shape=(out, out),
        grid=(width // block,),
        in_specs=[pl.BlockSpec((count, block), lambda i: (0, i)), whole, whole],
        out_specs=(part, part),
        cost_estimate=SMALL,
        compiler_params=pltpu.CompilerParams(vmem_limit_bytes=40 << 20),
        name="x_terms",
    )(x_rows, gate_grad, up_grad)


def row_kernel(gate_ref, up_ref, w_ref, out_ref):
    half = gate_ref.shape[1]
    total = lax.dot_general(
        gate_ref[...], w_ref[:, :half], (((1,), (1,)), ((), ())), preferred_element_type=f32
    )
    total += lax.dot_general(
        up_ref[...], w_ref[:, half:], (((1,), (1,)), ((), ())), preferred_element_type=f32
    )
    out_ref[...] = total.astype(bf16)


def input_rows(gate_grad, up_grad, w_gate_up):
    count, n = gate_grad.shape
    width = w_gate_up.shape[0]
    block = block_of(width)
    whole = pl.BlockSpec((count, n), lambda i: (0, 0))
    return pl.pallas_call(
        row_kernel,
        out_shape=jax.ShapeDtypeStruct((count, width), bf16),
        grid=(width // block,),
        in_specs=[whole, whole, pl.BlockSpec((block, 2 * n), lambda i: (i, 0))],
        out_specs=pl.BlockSpec((count, block), lambda i: (0, i)),
        cost_estimate=SMALL,
        compiler_params=pltpu.CompilerParams(vmem_limit_bytes=40 << 20),
        name="input_rows",
    )(gate_grad, up_grad, w_gate_up)


def put_kernel(count, rows_ref, *refs):
    pieces, out_ref, sems = refs[:count], refs[-2], refs[-1]
    copies = [
        pltpu.make_async_copy(
            piece,
            out_ref.at[pl.ds(pl.multiple_of(rows_ref[i], 16), piece.shape[0])],
            sems.at[i],
        )
        for i, piece in enumerate(pieces)
    ]
    for copy in copies:
        copy.start()
    for copy in copies:
        copy.wait()


def put(whole, height, placed):
    pieces = [piece for piece, _ in placed]
    count = len(pieces)
    starts = jnp.stack([row for _, row in placed]).astype(jnp.int32)
    old = [] if whole is None else [whole]
    out = jax.ShapeDtypeStruct((height, pieces[0].shape[1]), bf16)
    moved = sum(piece.size for piece in pieces) * 4
    return pl.pallas_call(
        lambda *refs: put_kernel(count, *refs),
        out_shape=out,
        in_specs=[pl.BlockSpec(memory_space=pltpu.SMEM)]
        + vmem_specs(count)
        + [pl.BlockSpec(memory_space=pl.ANY) for _ in old],
        out_specs=pl.BlockSpec(memory_space=pl.ANY),
        scratch_shapes=[pltpu.SemaphoreType.DMA((count,))],
        input_output_aliases={1 + count: 0} if old else {},
        cost_estimate=pl.CostEstimate(flops=0, transcendentals=0, bytes_accessed=moved),
        compiler_params=pltpu.CompilerParams(vmem_limit_bytes=40 << 20),
        name="put_rows",
    )(starts, *pieces, *old)


def neighbours(part):
    return lax.ppermute(part, "x", PLUS), lax.ppermute(part, "x", MINUS)


def far(left, right, half):
    return lax.ppermute(left[:half], "x", PLUS), lax.ppermute(right[half:], "x", MINUS)


def plus(*values):
    return sum(v.astype(f32) for v in values).astype(bf16)


def send(pair):
    to_right, to_left = pair
    return lax.ppermute(to_right, "x", PLUS), lax.ppermute(to_left, "x", MINUS)


class Scatter:
    def __init__(self, terms, x, yh):
        self.terms, self.x, self.yh = terms, x, yh
        self.size, self.n = terms.shape[0] // 8, terms.shape[1]

    def rows(self, k, side, count):
        start = self.size * (2 * ((self.x + k) % 4) + side)
        return lax.dynamic_slice(self.terms, (start, 0), (count * self.size, self.n))

    def first(self):
        to_right = jnp.concatenate((self.rows(2, 0, 1), self.rows(1, 1, 1)))
        to_left = jnp.concatenate((self.rows(2, 1, 1), self.rows(3, 0, 1)))
        return to_right, to_left

    def second(self, got):
        from_left, from_right = got
        self.low, self.top = from_left[self.size :], from_right[self.size :]
        to_right = plus(self.rows(1, 0, 1), from_left[: self.size])
        to_left = plus(self.rows(3, 1, 1), from_right[: self.size])
        return to_right, to_left

    def mine(self, side):
        top, low = self.got
        return plus(
            self.rows(0, side, 1),
            jnp.where(side == 0, top, self.low),
            jnp.where(side == 0, self.top, low),
        )

    def third(self):
        self.kept = self.mine(self.yh)
        return lax.ppermute(self.mine(1 - self.yh), "yh", SWAP)

    def last(self, sent):
        return plus(self.kept, sent)


def body(
    layer_input,
    output_grad,
    expert_ids,
    gate_probs,
    gate_weight,
    up_weight,
    down_weight,
    gate_moment,
    up_moment,
    down_moment,
    gate_second,
    up_second,
    down_second,
):
    x, yh, yl = lax.axis_index("x"), lax.axis_index("yh"), lax.axis_index("yl")
    z, c = lax.axis_index("z"), lax.axis_index("c")
    tok, picks = expert_ids.shape
    capacity = 3 * tok * picks // (2 * GROUPS)
    width = layer_input.shape[1]
    hidden_units = gate_weight.shape[2]
    quarter = hidden_units // 4
    half = hidden_units // 2
    rows = GROUPS * capacity
    depth = gate_weight.shape[1]

    gate_low, up_low = gate_weight[0].astype(bf16), up_weight[0].astype(bf16)

    def chunk(core):
        cuts = [
            w[:, (core + 2 * k) * quarter : (core + 2 * k + 1) * quarter]
            for w in (gate_low, up_low)
            for k in range(2)
        ]
        return jnp.concatenate(cuts, axis=1)

    chunks = (chunk(0), chunk(1))
    part_a = lax.ppermute(jnp.where(yl == 0, chunks[0], chunks[1]), ("yl", "c"), PAIR_A)
    part_b = lax.ppermute(jnp.where(yl == 0, chunks[1], chunks[0]), ("yl", "c"), PAIR_B)
    down_part = lax.ppermute(down_weight[0].astype(bf16), CYCLE_AXES, CYCLE)
    part_a, part_b, down_part = join((part_a, part_b, down_part))
    part = jnp.where(
        c == 0, jnp.concatenate((part_a, part_b)), jnp.concatenate((part_b, part_a))
    )

    part_other = lax.ppermute(part, "yh", SWAP)
    down_other = lax.ppermute(down_part, "yh", SWAP)
    near_own = join(neighbours(part))
    far_own = far(*near_own, depth)
    ids = expert_ids.T
    sent = pack_rows(ids, gate_probs.T.astype(f32), layer_input, output_grad, capacity)
    sent, part_other, down_other, far_own = join((sent, part_other, down_other, far_own))

    size_down = down_part.shape[0]
    both = jnp.where(
        yh == 0,
        jnp.concatenate((down_part, down_other)),
        jnp.concatenate((down_other, down_part)),
    )

    def gate_up_row(k, side):
        return 2 * depth * (2 * ((x + k) % 4) + side)

    def down_row(k):
        return 2 * size_down * ((x + k) % 4)

    def ring_rows(row, part, left, right):
        return [(part, row(0)), (left, row(3)), (right, row(1))]

    def far_rows_of(row, top, low):
        return [(top, row(2)), (low, row(2) + top.shape[0])]

    own_row = lambda k: gate_up_row(k, yh)
    other_row = lambda k: gate_up_row(k, 1 - yh)
    near_other = neighbours(part_other)
    own = lax.all_to_all(
        sent.reshape(GROUPS, capacity, -1), ("yl", "z"), 0, 0, tiled=True
    ).reshape(rows, -1)
    w_gate_up = put(
        None,
        width,
        ring_rows(own_row, part, *near_own) + far_rows_of(own_row, *far_own),
    )
    near_other, w_gate_up, both = join((near_other, w_gate_up, both))
    near_down = neighbours(both)
    far_other = far(*near_other, depth)
    w_gate_up = put(w_gate_up, width, ring_rows(other_row, part_other, *near_other))
    own, near_down, far_other, w_gate_up = join((own, near_down, far_other, w_gate_up))
    far_down = far(*near_down, size_down)
    w_gate_up = put(w_gate_up, width, far_rows_of(other_row, *far_other))
    w_down = put(None, half, ring_rows(down_row, both, *near_down))
    other = lax.ppermute(own, "c", SWAP)
    x_rows = jnp.concatenate((own[:, :width], other[:, :width]))
    y_rows = jnp.concatenate((own[:, width : 2 * width], other[:, width : 2 * width]))
    gates = jnp.concatenate((own[:, 2 * width :], other[:, 2 * width :]))[:, :1].astype(f32)

    pre = jnp.dot(x_rows, w_gate_up, preferred_element_type=f32)
    gate_pre, up_pre = pre[:, :half], pre[:, half:]
    sigmoid_gate = jax.nn.sigmoid(gate_pre)
    silu_gate = gate_pre * sigmoid_gate
    hidden_full = silu_gate * up_pre
    hidden = hidden_full.astype(bf16)
    hidden_scaled = (gates * hidden_full).astype(bf16)
    down_term = lax.dot_general(
        hidden_scaled, y_rows, (((0,), (0,)), ((), ())), preferred_element_type=f32
    ).astype(bf16)
    down_sum = Scatter(down_term, x, yh)
    down_send = down_sum.first()
    far_down, down_send = join((far_down, down_send))
    w_down = put(w_down, half, far_rows_of(down_row, *far_down))
    down_got = send(down_send)
    raw_grad = lax.dot_general(
        y_rows, w_down, (((1,), (1,)), ((), ())), preferred_element_type=f32
    )
    prob_rows = jnp.sum(hidden.astype(f32) * raw_grad, axis=1, keepdims=True)
    hidden_grad = gates * raw_grad
    dsilu = sigmoid_gate * (1.0 + gate_pre * (1.0 - sigmoid_gate))
    gate_grad = (hidden_grad * up_pre * dsilu).astype(bf16)
    up_grad = (hidden_grad * silu_gate).astype(bf16)

    gate_term, up_term = x_terms(x_rows, gate_grad, up_grad)
    gate_sum, up_sum = Scatter(gate_term, x, yh), Scatter(up_term, x, yh)

    far_part = input_rows(gate_grad[rows:], up_grad[rows:], w_gate_up)
    far_prob = jnp.broadcast_to(prob_rows[rows:], (rows, LANES))
    far_prob = lax.ppermute(far_prob, "c", SWAP)
    gate_send = gate_sum.first()
    down_got, gate_send, far_part, far_prob = join((down_got, gate_send, far_part, far_prob))
    down_send = down_sum.second(down_got)
    gate_grad, up_grad, down_send, gate_send = join(
        (gate_grad, up_grad, down_send, gate_send)
    )
    down_got, gate_got = send(down_send), send(gate_send)
    far_rows = lax.ppermute(far_part, "c", SWAP)
    near_rows = (
        input_rows(gate_grad[:rows], up_grad[:rows], w_gate_up).astype(f32)
        + far_rows.astype(f32)
    ).astype(bf16)
    near_prob = (prob_rows[:rows] + far_prob).astype(bf16)
    packed = jnp.concatenate((near_rows, near_prob), axis=1)
    gate_got, down_sum.got = join((gate_got, down_got))
    gate_send, up_send = join((gate_sum.second(gate_got), up_sum.first()))
    gate_got, up_got = send(gate_send), send(up_send)
    down_sent = down_sum.third()
    returned = lax.all_to_all(
        packed.reshape(GROUPS, capacity, -1), ("yl", "z"), 0, 0, tiled=True
    ).reshape(rows, -1)
    up_got, gate_sum.got, down_sent, returned = join((up_got, gate_got, down_sent, returned))

    def send_home(grad):
        return tuple(
            lax.ppermute(
                lax.dynamic_slice(grad, (depth * start, 0), (depth, half)),
                ("yl", "c"),
                back(pairs),
            )
            for start, pairs in ((c, PAIR_A), (1 - c, PAIR_B))
        )

    def natural(home):
        even = jnp.where(yl == 0, home[0], home[1])
        odd = jnp.where(yl == 0, home[1], home[0])
        return jnp.concatenate(
            [v[:, k * quarter : (k + 1) * quarter] for k in range(2) for v in (even, odd)],
            axis=1,
        )[None].astype(f32)

    down_home = down_sum.last(down_sent)
    up_send, gate_sum.got, down_home = join((up_sum.second(up_got), gate_sum.got, down_home))
    up_got = send(up_send)
    gate_sent = gate_sum.third()
    down_home = lax.ppermute(down_home, CYCLE_AXES, back(CYCLE))
    up_sum.got, gate_sent, down_home = join((up_got, gate_sent, down_home))
    up_mine, gate_sent = join((up_sum.mine(1 - yh), gate_sent))
    up_sent = lax.ppermute(up_mine, "yh", SWAP)
    up_sum.kept = up_sum.mine(yh)
    gate_home = send_home(gate_sum.last(gate_sent))
    new_down_weight, new_down_moment, new_down_second = adamw(
        down_weight, down_moment, down_second, down_home.astype(f32)[None]
    )
    up_sent, gate_home = join((up_sent, gate_home))
    up_home = send_home(up_sum.last(up_sent))
    input_grad, prob_grad = unpack_rows(ids, returned, width, capacity)
    new_gate_weight, new_gate_moment, new_gate_second = adamw(
        gate_weight, gate_moment, gate_second, natural(gate_home)
    )
    up_home, new_gate_weight = join((up_home, new_gate_weight))
    new_up_weight, new_up_moment, new_up_second = adamw(
        up_weight, up_moment, up_second, natural(up_home)
    )
    return (
        input_grad,
        prob_grad.T,
        new_gate_weight,
        new_up_weight,
        new_down_weight,
        new_gate_moment,
        new_up_moment,
        new_down_moment,
        new_gate_second,
        new_up_second,
        new_down_second,
    )


def solution(mesh):
    fine = Mesh(mesh.devices.reshape(4, 2, 2, 4, 2), ("x", "yh", "yl", "z", "c"))
    tokens = P(("x", "yh", "yl", "z", "c"), None)
    weights = P(("z", "c"), ("x", "yh", "yl"), None)
    return jax.shard_map(
        body,
        mesh=fine,
        in_specs=(tokens,) * 4 + (weights,) * 9,
        out_specs=(tokens,) * 2 + (weights,) * 9,
        check_vma=False,
    )
```

profile of v0, /device:TPU:1, one launch (start us, length us, event | category | flops | bytes accessed | tf_op | source)
XLA Modules:
  0.0 356.3 jit_solution(2617377157118646055)
XLA Ops:
  3.5 4.6 %collective-permute-start = (bf16[160,1536]{1,0:T(8,128)(2,1)S(1)}, bf16[160,1536]{1,0:T(8,128)(2,1)S(1)}, u32[]{:S(2)}, u32[]{:S(2)}) collective-permute-start(bf16[160,1536]{1,0:T(8,128)(2,1)S(1)} %get-tuple-element.188), channel_id=1, source_target_pairs={{0,0},{1,8},{8,1},{9,9},{2,2},{3,10},{10,3},{11,11},{4,4},{5,12},{... | collective-permute-start | bytes 1474568 | tf_op jit(solution)/shard_map/ppermute | solution.py:343
  10.3 7.6 %collective-permute-done = bf16[160,1536]{1,0:T(8,128)(2,1)S(1)} collective-permute-done((bf16[160,1536]{1,0:T(8,128)(2,1)S(1)}, bf16[160,1536]{1,0:T(8,128)(2,1)S(1)}, u32[]{:S(2)}, u32[]{:S(2)}) %collective-permute-start) | collective-permute-done | bytes 491552 | tf_op jit(solution)/shard_map/ppermute | solution.py:343
  17.9 6.6 %collective-permute-done.1 = bf16[160,1536]{1,0:T(8,128)(2,1)S(1)} collective-permute-done((bf16[160,1536]{1,0:T(8,128)(2,1)S(1)}, bf16[160,1536]{1,0:T(8,128)(2,1)S(1)}, u32[]{:S(2)}, u32[]{:S(2)}) %collective-permute-start.1) | collective-permute-done | bytes 491552 | tf_op jit(solution)/shard_map/ppermute | solution.py:344
  24.4 5.3 %collective-permute-done.2 = bf16[96,2560]{1,0:T(8,128)(2,1)} collective-permute-done((bf16[96,2560]{1,0:T(8,128)(2,1)S(1)}, bf16[96,2560]{1,0:T(8,128)(2,1)}, u32[]{:S(2)}, u32[]{:S(2)}) %collective-permute-start.2) | collective-permute-done | bytes 491552 | tf_op jit(solution)/shard_map/ppermute | solution.py:345
  33.6 2.7 collective-permute-start.3
  36.6 18.1 %collective-permute-done.5.refs_2_ = bf16[320,1536]{1,0:T(8,128)(2,1)S(1)} collective-permute-done((bf16[320,1536]{1,0:T(8,128)(2,1)S(1)}, bf16[320,1536]{1,0:T(8,128)(2,1)S(1)}, u32[]{:S(2)}, u32[]{:S(2)}) %collective-permute-start.5) | collective-permute-done | bytes 983072 | tf_op jit(solution)/shard_map/ppermute | solution.py:253
  55.6 2.7 collective-permute-start.8
  64.4 3.3 collective-permute-done.4
  69.6 5.3 %all-to-all-start = ((bf16[8,48,5248]{2,1,0:T(8,128)(2,1)}), bf16[8,48,5248]{2,1,0:T(8,128)(2,1)}, u32[]{:S(2)}, u32[]{:S(2)}) async-start(bf16[8,48,5248]{2,1,0:T(8,128)(2,1)} %bitcast.57), calls=%async_computation | async-start | bytes 8060928 | tf_op jit(solution)/shard_map/all_to_all | solution.py:381
  80.7 3.1 copy-done
  85.3 11.7 %collective-permute-done.10.refs_3_ = bf16[320,1536]{1,0:T(8,128)(2,1)} collective-permute-done((bf16[320,1536]{1,0:T(8,128)(2,1)}, bf16[320,1536]{1,0:T(8,128)(2,1)}, u32[]{:S(2)}, u32[]{:S(2)}) %collective-permute-start.10) | collective-permute-done | bytes 983072 | tf_op jit(solution)/shard_map/ppermute | solution.py:253
  97.0 3.1 collective-permute-done.9.refs_2_
  100.1 2.7 collective-permute-start.12
  106.5 2.7 collective-permute-start.14
  109.3 3.2 copy-done.1
  116.2 3.1 copy-done.2
  119.3 12.8 %collective-permute-done.13.refs_1_ = bf16[160,1536]{1,0:T(8,128)(2,1)S(1)} collective-permute-done((bf16[160,1536]{1,0:T(8,128)(2,1)}, bf16[160,1536]{1,0:T(8,128)(2,1)S(1)}, u32[]{:S(2)}, u32[]{:S(2)}) %collective-permute-start.13) | collective-permute-done | bytes 491552 | tf_op jit(solution)/shard_map/ppermute | solution.py:257
  132.2 4.0 %collective-permute-start.15 = (bf16[384,5248]{1,0:T(8,128)(2,1)}, bf16[384,5248]{1,0:T(8,128)(2,1)}, u32[]{:S(2)}, u32[]{:S(2)}) collective-permute-start(bf16[384,5248]{1,0:T(8,128)(2,1)} %bitcast.6), channel_id=1, source_target_pairs={{0,1},{1,0},{2,3},{3,2},{4,5},{5,4},{6,7},{7,6},{8,9},{9,8},{10,11... | collective-permute-start | bytes 12091400 | tf_op jit(solution)/shard_map/ppermute | solution.py:397
  140.4 3.0 collective-permute-start.17
  145.2 5.2 %fusion.21 = (bf16[384,2560]{1,0:T(8,128)(2,1)S(1)}, bf16[384,2560]{1,0:T(8,128)(2,1)S(1)}) fusion(bf16[384,5248]{1,0:T(8,128)(2,1)} %bitcast.6), kind=kLoop, calls=%fused_computation.102 | loop fusion | bytes 7864320 | tf_op jit(solution)/shard_map/slice | solution.py:399
  154.0 8.6 %fusion.13 = f32[768,1536]{1,0:T(8,128)} fusion(bf16[2560,1536]{1,0:T(8,128)(2,1)S(1)} %put_rows.7.w_ref, bf16[384,2560]{1,0:T(8,128)(2,1)S(1)} %get-tuple-element.168, bf16[384,2560]{1,0:T(8,128)(2,1)S(1)} %get-tuple-element.166), kind=kOutput, calls=%fused_computation.101 | convolution fusion | flops 6047662080 | bytes 16515072 | tf_op jit(solution)/shard_map/dot_general | solution.py:402
  162.6 5.8 %convolution_convert_fusion = bf16[768,2560]{1,0:T(8,128)(2,1)S(1)} fusion(bf16[384,2560]{1,0:T(8,128)(2,1)S(1)} %get-tuple-element.167, bf16[384,2560]{1,0:T(8,128)(2,1)S(1)} %get-tuple-element.165, f32[768]{0:T(1024)S(1)} %convert_reduce_fusion, f32[768,1536]{1,0:T(8,128)} %fusion.13), kind=kOutput, calls=%fused_computation | convolution fusion | flops 3033858048 | bytes 12585984 | tf_op jit(solution)/shard_map/dot_general | solution.py:409
  173.8 7.0 %multiply_convert_fusion = (bf16[768,768]{1,0:T(8,128)(2,1)S(1)}, bf16[768,768]{1,0:T(8,128)(2,1)S(1)}, f32[768]{0:T(1024)S(1)}) fusion(f32[768]{0:T(1024)S(1)} %convert_reduce_fusion, f32[768,1536]{1,0:T(8,128)} %fusion.13, bf16[768,2560]{1,0:T(8,128)(2,1)S(1)} %put_rows.9, bf16[384,2560]{1,0:T(8,128)(2,1)S(1)} %copy-done.24, ...), kind=kOutput, calls=%fused_computation.6 | convolution fusion | flops 3038969088 | bytes 14948352 | tf_op jit(solution)/shard_map/dot_general | solution.py:417
  180.9 2.7 collective-permute-start.19
  183.8 7.4 %x_terms.1 = (bf16[2560,768]{1,0:T(8,128)(2,1)S(1)}, bf16[2560,768]{1,0:T(8,128)(2,1)S(1)}) custom-call(bf16[768,2560]{1,0:T(8,128)(2,1)S(1)} %pad_maximum_fusion.x_ref, bf16[768,768]{1,0:T(8,128)(2,1)S(1)} %get-tuple-element.124.gate_ref, bf16[768,768]{1,0:T(8,128)(2,1)S(1)} %get-tuple-element.125.up_ref), custom_call_target="tpu_custom_call" | custom-call | flops 1 | bytes 1 | tf_op jit(solution)/shard_map/x_terms/pallas_call | solution.py:174
  194.8 4.8 %input_rows.2 = bf16[384,2560]{1,0:T(8,128)(2,1)} custom-call(bf16[384,768]{1,0:T(8,128)(2,1)S(1)} %slice.211.gate_ref, bf16[384,768]{1,0:T(8,128)(2,1)S(1)} %slice.212.up_ref, bf16[2560,1536]{1,0:T(8,128)(2,1)S(1)} %put_rows.7.w_ref), custom_call_target="tpu_custom_call" | custom-call | flops 1 | bytes 1 | tf_op jit(solution)/shard_map/input_rows/pallas_call | solution.py:202
  200.7 4.6 %collective-permute-done.18 = bf16[192,2560]{1,0:T(8,128)(2,1)S(1)} collective-permute-done((bf16[192,2560]{1,0:T(8,128)(2,1)}, bf16[192,2560]{1,0:T(8,128)(2,1)S(1)}, u32[]{:S(2)}, u32[]{:S(2)}) %collective-permute-start.18) | collective-permute-done | bytes 983072 | tf_op jit(solution)/shard_map/ppermute | solution.py:266
  209.2 2.9 collective-permute-start.22
  212.0 2.7 collective-permute-start.24
  214.7 3.2 copy-done.5
  217.9 4.1 %input_rows.3 = bf16[384,2560]{1,0:T(8,128)(2,1)S(1)} custom-call(bf16[384,768]{1,0:T(8,128)(2,1)S(1)} %slice.181.gate_ref, bf16[384,768]{1,0:T(8,128)(2,1)S(1)} %slice.182.up_ref, bf16[2560,1536]{1,0:T(8,128)(2,1)S(1)} %copy-done.5), custom_call_target="tpu_custom_call" | custom-call | flops 1 | bytes 1 | tf_op jit(solution)/shard_map/input_rows/pallas_call | solution.py:202
  225.8 4.9 %all-to-all-start.1 = ((bf16[8,48,2688]{2,1,0:T(8,128)(2,1)}), bf16[8,48,2688]{2,1,0:T(8,128)(2,1)S(1)}, u32[]{:S(2)}, u32[]{:S(2)}) async-start(bf16[8,48,2688]{2,1,0:T(8,128)(2,1)} %bitcast.61), calls=%async_computation.1 | async-start | bytes 4128768 | tf_op jit(solution)/shard_map/all_to_all | solution.py:450
  234.3 10.6 %collective-permute-done.23 = bf16[96,2560]{1,0:T(8,128)(2,1)} collective-permute-done((bf16[96,2560]{1,0:T(8,128)(2,1)}, bf16[96,2560]{1,0:T(8,128)(2,1)}, u32[]{:S(2)}, u32[]{:S(2)}) %collective-permute-start.23) | collective-permute-done | bytes 491552 | tf_op jit(solution)/shard_map/ppermute | solution.py:266
  244.8 2.7 add_convert_fusion.12
  252.6 3.5 collective-permute-start.29
  256.2 2.7 collective-permute-start.28
  258.8 8.4 %collective-permute-done.29 = bf16[96,2560]{1,0:T(8,128)(2,1)} collective-permute-done((bf16[96,2560]{1,0:T(8,128)(2,1)}, bf16[96,2560]{1,0:T(8,128)(2,1)}, u32[]{:S(2)}, u32[]{:S(2)}) %collective-permute-start.29) | collective-permute-done | bytes 491552 | tf_op jit(solution)/shard_map/ppermute | solution.py:300
  267.2 15.0 %collective-permute-done.27 = bf16[320,768]{1,0:T(8,128)(2,1)} collective-permute-done((bf16[320,768]{1,0:T(8,128)(2,1)}, bf16[320,768]{1,0:T(8,128)(2,1)}, u32[]{:S(2)}, u32[]{:S(2)}) %collective-permute-start.27) | collective-permute-done | bytes 491552 | tf_op jit(solution)/shard_map/ppermute | solution.py:266
  282.2 2.7 add_convert_fusion.7
  290.1 3.5 collective-permute-start.33
  296.3 3.7 %collective-permute-start.34 = (bf16[96,2560]{1,0:T(8,128)(2,1)}, bf16[96,2560]{1,0:T(8,128)(2,1)}, u32[]{:S(2)}, u32[]{:S(2)}) collective-permute-start(bf16[96,2560]{1,0:T(8,128)(2,1)} %add_convert_fusion.7), channel_id=1, source_target_pairs={{0,0},{8,1},{16,8},{24,9},{32,16},{40,17},{48,24},{56,25},{1,32},{... | collective-permute-start | bytes 1474568 | tf_op jit(solution)/shard_map/ppermute | solution.py:477
  305.9 5.3 %collective-permute-done.34 = bf16[96,2560]{1,0:T(8,128)(2,1)} collective-permute-done((bf16[96,2560]{1,0:T(8,128)(2,1)}, bf16[96,2560]{1,0:T(8,128)(2,1)}, u32[]{:S(2)}, u32[]{:S(2)}) %collective-permute-start.34) | collective-permute-done | bytes 491552 | tf_op jit(solution)/shard_map/ppermute | solution.py:477
  315.0 7.8 %collective-permute-start.36 = (bf16[160,768]{1,0:T(8,128)(2,1)S(1)}, bf16[160,768]{1,0:T(8,128)(2,1)S(1)}, u32[]{:S(2)}, u32[]{:S(2)}) collective-permute-start(bf16[160,768]{1,0:T(8,128)(2,1)S(1)} %get-tuple-element.196), channel_id=1, source_target_pairs={{0,0},{8,1},{1,8},{9,9},{2,2},{10,3},{3,10},{11,11},{4,4},{12,5},{... | collective-permute-start | bytes 737288 | tf_op jit(solution)/shard_map/ppermute | solution.py:457
  322.9 2.8 collective-permute-start.35
  325.7 3.1 multiply_subtract_fusion
  330.1 9.7 %collective-permute-done.35 = bf16[320,768]{1,0:T(8,128)(2,1)S(1)} collective-permute-done((bf16[320,768]{1,0:T(8,128)(2,1)S(1)}, bf16[320,768]{1,0:T(8,128)(2,1)S(1)}, u32[]{:S(2)}, u32[]{:S(2)}) %collective-permute-start.35) | collective-permute-done | bytes 491552 | tf_op jit(solution)/shard_map/ppermute | solution.py:480
  341.9 5.6 %collective-permute-start.38 = (bf16[160,768]{1,0:T(8,128)(2,1)S(1)}, bf16[160,768]{1,0:T(8,128)(2,1)S(1)}, u32[]{:S(2)}, u32[]{:S(2)}) collective-permute-start(bf16[160,768]{1,0:T(8,128)(2,1)S(1)} %get-tuple-element.194), channel_id=1, source_target_pairs={{0,0},{8,1},{1,8},{9,9},{2,2},{10,3},{3,10},{11,11},{4,4},{12,5},{... | collective-permute-start | bytes 737288 | tf_op jit(solution)/shard_map/ppermute | solution.py:457
  349.8 2.9 collective-permute-done.38
  (179 shorter events, 95.3 us)
Async XLA Ops:
  3.5 14.3 %collective-permute-start = (bf16[160,1536]{1,0:T(8,128)(2,1)S(1)}, bf16[160,1536]{1,0:T(8,128)(2,1)S(1)}, u32[]{:S(2)}, u32[]{:S(2)}) collective-permute-start(bf16[160,1536]{1,0:T(8,128)(2,1)S(1)} %get-tuple-element.188), channel_id=1, source_target_pairs={{0,0},{1,8},{8,1},{9,9},{2,2},{3,10},{10,3},{11,11},{4,4},{5,12},{... | collective-permute-start | bytes 1474568 | tf_op jit(solution)/shard_map/ppermute | solution.py:343
  8.2 50.1 %copy-start.33 = (bf16[128,2]{0,1:T(2,128)(2,1)S(1)}, bf16[128,2]{0,1:T(2,128)(2,1)}, u32[]{:S(2)}) copy-start(bf16[128,2]{0,1:T(2,128)(2,1)} %param.16) | copy-start | bytes 1540
  8.2 50.1 %copy-start.15 = (s32[128,2]{0,1:T(2,128)S(1)}, s32[128,2]{0,1:T(2,128)}, u32[]{:S(2)}) copy-start(s32[128,2]{0,1:T(2,128)} %param.15) | copy-start | bytes 3076
  8.2 16.3 %collective-permute-start.1 = (bf16[160,1536]{1,0:T(8,128)(2,1)S(1)}, bf16[160,1536]{1,0:T(8,128)(2,1)S(1)}, u32[]{:S(2)}, u32[]{:S(2)}) collective-permute-start(bf16[160,1536]{1,0:T(8,128)(2,1)S(1)} %get-tuple-element.187), channel_id=1, source_target_pairs={{0,1},{1,9},{8,0},{9,8},{2,3},{3,11},{10,2},{11,10},{4,5},{5,13},{... | collective-permute-start | bytes 1474568 | tf_op jit(solution)/shard_map/ppermute | solution.py:344
  8.3 21.4 %collective-permute-start.2 = (bf16[96,2560]{1,0:T(8,128)(2,1)S(1)}, bf16[96,2560]{1,0:T(8,128)(2,1)}, u32[]{:S(2)}, u32[]{:S(2)}) collective-permute-start(bf16[96,2560]{1,0:T(8,128)(2,1)S(1)} %convert_bitcast_fusion), channel_id=1, source_target_pairs={{0,0},{1,8},{8,16},{9,24},{16,32},{17,40},{24,48},{25,56},{32,1},{... | collective-permute-start | bytes 1474568 | tf_op jit(solution)/shard_map/ppermute | solution.py:345
  30.0 24.7 %collective-permute-start.5 = (bf16[320,1536]{1,0:T(8,128)(2,1)S(1)}, bf16[320,1536]{1,0:T(8,128)(2,1)S(1)}, u32[]{:S(2)}, u32[]{:S(2)}) collective-permute-start(bf16[320,1536]{1,0:T(8,128)(2,1)S(1)} %maximum_select_fusion.refs_1_), channel_id=1, source_target_pairs={{0,32},{32,64},{64,96},{96,0},{1,33},{33,65},{65,97},{97,1},{2,34}... | collective-permute-start | bytes 2949128 | tf_op jit(solution)/shard_map/ppermute | solution.py:253
  32.2 23.2 %collective-permute-start.6 = (bf16[320,1536]{1,0:T(8,128)(2,1)S(1)}, bf16[320,1536]{1,0:T(8,128)(2,1)S(1)}, u32[]{:S(2)}, u32[]{:S(2)}) collective-permute-start(bf16[320,1536]{1,0:T(8,128)(2,1)S(1)} %maximum_select_fusion.refs_1_), channel_id=1, source_target_pairs={{0,96},{32,0},{64,32},{96,64},{1,97},{33,1},{65,33},{97,65},{2,98}... | collective-permute-start | bytes 2949128 | tf_op jit(solution)/shard_map/ppermute | solution.py:253
  33.6 34.2 %collective-permute-start.3 = (bf16[320,1536]{1,0:T(8,128)(2,1)S(1)}, bf16[320,1536]{1,0:T(8,128)(2,1)S(1)}, u32[]{:S(2)}, u32[]{:S(2)}) collective-permute-start(bf16[320,1536]{1,0:T(8,128)(2,1)S(1)} %maximum_select_fusion.refs_1_), channel_id=1, source_target_pairs={{0,16},{16,0},{1,17},{17,1},{2,18},{18,2},{3,19},{19,3},{4,20},{20... | collective-permute-start | bytes 2949128 | tf_op jit(solution)/shard_map/ppermute | solution.py:351
  36.2 31.5 %collective-permute-start.4 = (bf16[96,2560]{1,0:T(8,128)(2,1)}, bf16[96,2560]{1,0:T(8,128)(2,1)S(1)}, u32[]{:S(2)}, u32[]{:S(2)}) collective-permute-start(bf16[96,2560]{1,0:T(8,128)(2,1)} %collective-permute-done.2), channel_id=1, source_target_pairs={{0,16},{16,0},{1,17},{17,1},{2,18},{18,2},{3,19},{19,3},{4,20},{20... | collective-permute-start | bytes 1474568 | tf_op jit(solution)/shard_map/ppermute | solution.py:352
  55.4 13.3 %collective-permute-start.7 = (bf16[160,1536]{1,0:T(8,128)(2,1)S(1)}, bf16[160,1536]{1,0:T(8,128)(2,1)S(1)}, u32[]{:S(2)}, u32[]{:S(2)}) collective-permute-start(bf16[160,1536]{1,0:T(8,128)(2,1)S(1)} %slice.157), channel_id=1, source_target_pairs={{0,32},{32,64},{64,96},{96,0},{1,33},{33,65},{65,97},{97,1},{2,34}... | collective-permute-start | bytes 1474568 | tf_op jit(solution)/shard_map/ppermute | solution.py:257
  55.6 13.2 %collective-permute-start.8 = (bf16[160,1536]{1,0:T(8,128)(2,1)S(1)}, bf16[160,1536]{1,0:T(8,128)(2,1)S(1)}, u32[]{:S(2)}, u32[]{:S(2)}) collective-permute-start(bf16[160,1536]{1,0:T(8,128)(2,1)S(1)} %slice.158), channel_id=1, source_target_pairs={{0,96},{32,0},{64,32},{96,64},{1,97},{33,1},{65,33},{97,65},{2,98}... | collective-permute-start | bytes 1474568 | tf_op jit(solution)/shard_map/ppermute | solution.py:257
  69.6 62.5 %all-to-all-start = ((bf16[8,48,5248]{2,1,0:T(8,128)(2,1)}), bf16[8,48,5248]{2,1,0:T(8,128)(2,1)}, u32[]{:S(2)}, u32[]{:S(2)}) async-start(bf16[8,48,5248]{2,1,0:T(8,128)(2,1)} %bitcast.57), calls=%async_computation | async-start | bytes 8060928 | tf_op jit(solution)/shard_map/all_to_all | solution.py:381
  74.9 22.1 %collective-permute-start.10 = (bf16[320,1536]{1,0:T(8,128)(2,1)}, bf16[320,1536]{1,0:T(8,128)(2,1)}, u32[]{:S(2)}, u32[]{:S(2)}) collective-permute-start(bf16[320,1536]{1,0:T(8,128)(2,1)} %copy-done.9), channel_id=1, source_target_pairs={{0,96},{32,0},{64,32},{96,64},{1,97},{33,1},{65,33},{97,65},{2,98}... | collective-permute-start | bytes 2949128 | tf_op jit(solution)/shard_map/ppermute | solution.py:253
  77.4 22.7 %collective-permute-start.9 = (bf16[320,1536]{1,0:T(8,128)(2,1)}, bf16[320,1536]{1,0:T(8,128)(2,1)}, u32[]{:S(2)}, u32[]{:S(2)}) collective-permute-start(bf16[320,1536]{1,0:T(8,128)(2,1)} %copy-done.9), channel_id=1, source_target_pairs={{0,32},{32,64},{64,96},{96,0},{1,33},{33,65},{65,97},{97,1},{2,34}... | collective-permute-start | bytes 2949128 | tf_op jit(solution)/shard_map/ppermute | solution.py:253
  100.1 32.0 %collective-permute-start.11 = (bf16[192,2560]{1,0:T(8,128)(2,1)S(1)}, bf16[192,2560]{1,0:T(8,128)(2,1)S(1)}, u32[]{:S(2)}, u32[]{:S(2)}) collective-permute-start(bf16[192,2560]{1,0:T(8,128)(2,1)S(1)} %maximum_select_fusion.1.refs_1_), channel_id=1, source_target_pairs={{0,32},{32,64},{64,96},{96,0},{1,33},{33,65},{65,97},{97,1},{2,34}... | collective-permute-start | bytes 2949128 | tf_op jit(solution)/shard_map/ppermute | solution.py:253
  100.1 32.0 %collective-permute-start.12 = (bf16[192,2560]{1,0:T(8,128)(2,1)S(1)}, bf16[192,2560]{1,0:T(8,128)(2,1)S(1)}, u32[]{:S(2)}, u32[]{:S(2)}) collective-permute-start(bf16[192,2560]{1,0:T(8,128)(2,1)S(1)} %maximum_select_fusion.1.refs_1_), channel_id=1, source_target_pairs={{0,96},{32,0},{64,32},{96,64},{1,97},{33,1},{65,33},{97,65},{2,98}... | collective-permute-start | bytes 2949128 | tf_op jit(solution)/shard_map/ppermute | solution.py:253
  104.7 27.5 %collective-permute-start.13 = (bf16[160,1536]{1,0:T(8,128)(2,1)}, bf16[160,1536]{1,0:T(8,128)(2,1)S(1)}, u32[]{:S(2)}, u32[]{:S(2)}) collective-permute-start(bf16[160,1536]{1,0:T(8,128)(2,1)} %slice.159), channel_id=1, source_target_pairs={{0,32},{32,64},{64,96},{96,0},{1,33},{33,65},{65,97},{97,1},{2,34}... | collective-permute-start | bytes 1474568 | tf_op jit(solution)/shard_map/ppermute | solution.py:257
  106.5 25.6 %collective-permute-start.14 = (bf16[160,1536]{1,0:T(8,128)(2,1)}, bf16[160,1536]{1,0:T(8,128)(2,1)}, u32[]{:S(2)}, u32[]{:S(2)}) collective-permute-start(bf16[160,1536]{1,0:T(8,128)(2,1)} %slice.160), channel_id=1, source_target_pairs={{0,96},{32,0},{64,32},{96,64},{1,97},{33,1},{65,33},{97,65},{2,98}... | collective-permute-start | bytes 1474568 | tf_op jit(solution)/shard_map/ppermute | solution.py:257
  132.2 18.3 %collective-permute-start.15 = (bf16[384,5248]{1,0:T(8,128)(2,1)}, bf16[384,5248]{1,0:T(8,128)(2,1)}, u32[]{:S(2)}, u32[]{:S(2)}) collective-permute-start(bf16[384,5248]{1,0:T(8,128)(2,1)} %bitcast.6), channel_id=1, source_target_pairs={{0,1},{1,0},{2,3},{3,2},{4,5},{5,4},{6,7},{7,6},{8,9},{9,8},{10,11... | collective-permute-start | bytes 12091400 | tf_op jit(solution)/shard_map/ppermute | solution.py:397
  140.3 31.3 %collective-permute-start.16 = (bf16[96,2560]{1,0:T(8,128)(2,1)}, bf16[96,2560]{1,0:T(8,128)(2,1)S(1)}, u32[]{:S(2)}, u32[]{:S(2)}) collective-permute-start(bf16[96,2560]{1,0:T(8,128)(2,1)} %slice.168), channel_id=1, source_target_pairs={{0,32},{32,64},{64,96},{96,0},{1,33},{33,65},{65,97},{97,1},{2,34}... | collective-permute-start | bytes 1474568 | tf_op jit(solution)/shard_map/ppermute | solution.py:257
  140.4 31.3 %collective-permute-start.17 = (bf16[96,2560]{1,0:T(8,128)(2,1)}, bf16[96,2560]{1,0:T(8,128)(2,1)S(1)}, u32[]{:S(2)}, u32[]{:S(2)}) collective-permute-start(bf16[96,2560]{1,0:T(8,128)(2,1)} %slice.169), channel_id=1, source_target_pairs={{0,96},{32,0},{64,32},{96,64},{1,97},{33,1},{65,33},{97,65},{2,98}... | collective-permute-start | bytes 1474568 | tf_op jit(solution)/shard_map/ppermute | solution.py:257
  145.2 49.6 %copy-start.4 = (bf16[2560,1536]{1,0:T(8,128)(2,1)}, bf16[2560,1536]{1,0:T(8,128)(2,1)S(1)}, u32[]{:S(2)}) copy-start(bf16[2560,1536]{1,0:T(8,128)(2,1)S(1)} %put_rows.7.w_ref) | copy-start | bytes 23592964
  180.8 24.5 %collective-permute-start.18 = (bf16[192,2560]{1,0:T(8,128)(2,1)}, bf16[192,2560]{1,0:T(8,128)(2,1)S(1)}, u32[]{:S(2)}, u32[]{:S(2)}) collective-permute-start(bf16[192,2560]{1,0:T(8,128)(2,1)} %pad_maximum_fusion.5), channel_id=1, source_target_pairs={{0,32},{32,64},{64,96},{96,0},{1,33},{33,65},{65,97},{97,1},{2,34}... | collective-permute-start | bytes 2949128 | tf_op jit(solution)/shard_map/ppermute | solution.py:266
  180.9 24.4 %collective-permute-start.19 = (bf16[192,2560]{1,0:T(8,128)(2,1)}, bf16[192,2560]{1,0:T(8,128)(2,1)}, u32[]{:S(2)}, u32[]{:S(2)}) collective-permute-start(bf16[192,2560]{1,0:T(8,128)(2,1)} %pad_maximum_fusion.6), channel_id=1, source_target_pairs={{0,96},{32,0},{64,32},{96,64},{1,97},{33,1},{65,33},{97,65},{2,98}... | collective-permute-start | bytes 2949128 | tf_op jit(solution)/shard_map/ppermute | solution.py:266
  191.5 9.2 %collective-permute-start.20 = (f32[384,128]{1,0:T(8,128)S(1)}, f32[384,128]{1,0:T(8,128)S(1)}, u32[]{:S(2)}, u32[]{:S(2)}) collective-permute-start(f32[384,128]{1,0:T(8,128)S(1)} %broadcast_in_dim.2), channel_id=1, source_target_pairs={{0,1},{1,0},{2,3},{3,2},{4,5},{5,4},{6,7},{7,6},{8,9},{9,8},{10,11... | collective-permute-start | bytes 589832 | tf_op jit(solution)/shard_map/ppermute | solution.py:431
  205.3 16.9 %collective-permute-start.30 = (bf16[384,2560]{1,0:T(8,128)(2,1)}, bf16[384,2560]{1,0:T(8,128)(2,1)}, u32[]{:S(2)}, u32[]{:S(2)}) collective-permute-start(bf16[384,2560]{1,0:T(8,128)(2,1)} %input_rows.2), channel_id=1, source_target_pairs={{0,1},{1,0},{2,3},{3,2},{4,5},{5,4},{6,7},{7,6},{8,9},{9,8},{10,11... | collective-permute-start | bytes 5898248 | tf_op jit(solution)/shard_map/ppermute | solution.py:439
  209.1 35.8 %collective-permute-start.21 = (bf16[640,768]{1,0:T(8,128)(2,1)}, bf16[640,768]{1,0:T(8,128)(2,1)}, u32[]{:S(2)}, u32[]{:S(2)}) collective-permute-start(bf16[640,768]{1,0:T(8,128)(2,1)} %pad_maximum_fusion.7), channel_id=1, source_target_pairs={{0,32},{32,64},{64,96},{96,0},{1,33},{33,65},{65,97},{97,1},{2,34}... | collective-permute-start | bytes 2949128 | tf_op jit(solution)/shard_map/ppermute | solution.py:266
  209.2 35.7 %collective-permute-start.22 = (bf16[640,768]{1,0:T(8,128)(2,1)}, bf16[640,768]{1,0:T(8,128)(2,1)}, u32[]{:S(2)}, u32[]{:S(2)}) collective-permute-start(bf16[640,768]{1,0:T(8,128)(2,1)} %pad_maximum_fusion.8), channel_id=1, source_target_pairs={{0,96},{32,0},{64,32},{96,64},{1,97},{33,1},{65,33},{97,65},{2,98}... | collective-permute-start | bytes 2949128 | tf_op jit(solution)/shard_map/ppermute | solution.py:266
  212.0 32.8 %collective-permute-start.23 = (bf16[96,2560]{1,0:T(8,128)(2,1)}, bf16[96,2560]{1,0:T(8,128)(2,1)}, u32[]{:S(2)}, u32[]{:S(2)}) collective-permute-start(bf16[96,2560]{1,0:T(8,128)(2,1)} %get-tuple-element.113), channel_id=1, source_target_pairs={{0,32},{32,64},{64,96},{96,0},{1,33},{33,65},{65,97},{97,1},{2,34}... | collective-permute-start | bytes 1474568 | tf_op jit(solution)/shard_map/ppermute | solution.py:266
  212.0 32.8 %collective-permute-start.24 = (bf16[96,2560]{1,0:T(8,128)(2,1)}, bf16[96,2560]{1,0:T(8,128)(2,1)}, u32[]{:S(2)}, u32[]{:S(2)}) collective-permute-start(bf16[96,2560]{1,0:T(8,128)(2,1)} %get-tuple-element.114), channel_id=1, source_target_pairs={{0,96},{32,0},{64,32},{96,64},{1,97},{33,1},{65,33},{97,65},{2,98}... | collective-permute-start | bytes 1474568 | tf_op jit(solution)/shard_map/ppermute | solution.py:266
  225.8 56.4 %all-to-all-start.1 = ((bf16[8,48,2688]{2,1,0:T(8,128)(2,1)}), bf16[8,48,2688]{2,1,0:T(8,128)(2,1)S(1)}, u32[]{:S(2)}, u32[]{:S(2)}) async-start(bf16[8,48,2688]{2,1,0:T(8,128)(2,1)} %bitcast.61), calls=%async_computation.1 | async-start | bytes 4128768 | tf_op jit(solution)/shard_map/all_to_all | solution.py:450
  247.5 34.7 %collective-permute-start.25 = (bf16[640,768]{1,0:T(8,128)(2,1)}, bf16[640,768]{1,0:T(8,128)(2,1)}, u32[]{:S(2)}, u32[]{:S(2)}) collective-permute-start(bf16[640,768]{1,0:T(8,128)(2,1)} %pad_maximum_fusion.9), channel_id=1, source_target_pairs={{0,32},{32,64},{64,96},{96,0},{1,33},{33,65},{65,97},{97,1},{2,34}... | collective-permute-start | bytes 2949128 | tf_op jit(solution)/shard_map/ppermute | solution.py:266
  248.2 34.0 %collective-permute-start.26 = (bf16[640,768]{1,0:T(8,128)(2,1)}, bf16[640,768]{1,0:T(8,128)(2,1)}, u32[]{:S(2)}, u32[]{:S(2)}) collective-permute-start(bf16[640,768]{1,0:T(8,128)(2,1)} %pad_maximum_fusion.10), channel_id=1, source_target_pairs={{0,96},{32,0},{64,32},{96,64},{1,97},{33,1},{65,33},{97,65},{2,98}... | collective-permute-start | bytes 2949128 | tf_op jit(solution)/shard_map/ppermute | solution.py:266
  252.6 14.5 %collective-permute-start.29 = (bf16[96,2560]{1,0:T(8,128)(2,1)}, bf16[96,2560]{1,0:T(8,128)(2,1)}, u32[]{:S(2)}, u32[]{:S(2)}) collective-permute-start(bf16[96,2560]{1,0:T(8,128)(2,1)} %add_convert_fusion.11), channel_id=1, source_target_pairs={{0,16},{16,0},{1,17},{17,1},{2,18},{18,2},{3,19},{19,3},{4,20},{20... | collective-permute-start | bytes 1474568 | tf_op jit(solution)/shard_map/ppermute | solution.py:300
  256.2 26.0 %collective-permute-start.27 = (bf16[320,768]{1,0:T(8,128)(2,1)}, bf16[320,768]{1,0:T(8,128)(2,1)}, u32[]{:S(2)}, u32[]{:S(2)}) collective-permute-start(bf16[320,768]{1,0:T(8,128)(2,1)} %get-tuple-element.120), channel_id=1, source_target_pairs={{0,32},{32,64},{64,96},{96,0},{1,33},{33,65},{65,97},{97,1},{2,34}... | collective-permute-start | bytes 1474568 | tf_op jit(solution)/shard_map/ppermute | solution.py:266
  256.2 26.0 %collective-permute-start.28 = (bf16[320,768]{1,0:T(8,128)(2,1)}, bf16[320,768]{1,0:T(8,128)(2,1)}, u32[]{:S(2)}, u32[]{:S(2)}) collective-permute-start(bf16[320,768]{1,0:T(8,128)(2,1)} %get-tuple-element.121), channel_id=1, source_target_pairs={{0,96},{32,0},{64,32},{96,64},{1,97},{33,1},{65,33},{97,65},{2,98}... | collective-permute-start | bytes 1474568 | tf_op jit(solution)/shard_map/ppermute | solution.py:266
  290.1 13.7 %collective-permute-start.33 = (bf16[320,768]{1,0:T(8,128)(2,1)}, bf16[320,768]{1,0:T(8,128)(2,1)S(1)}, u32[]{:S(2)}, u32[]{:S(2)}) collective-permute-start(bf16[320,768]{1,0:T(8,128)(2,1)} %add_convert_fusion.6), channel_id=1, source_target_pairs={{0,16},{16,0},{1,17},{17,1},{2,18},{18,2},{3,19},{19,3},{4,20},{20... | collective-permute-start | bytes 1474568 | tf_op jit(solution)/shard_map/ppermute | solution.py:300
  293.6 12.3 %collective-permute-start.31 = (bf16[320,768]{1,0:T(8,128)(2,1)}, bf16[320,768]{1,0:T(8,128)(2,1)S(1)}, u32[]{:S(2)}, u32[]{:S(2)}) collective-permute-start(bf16[320,768]{1,0:T(8,128)(2,1)} %get-tuple-element.136), channel_id=1, source_target_pairs={{0,32},{32,64},{64,96},{96,0},{1,33},{33,65},{65,97},{97,1},{2,34}... | collective-permute-start | bytes 1474568 | tf_op jit(solution)/shard_map/ppermute | solution.py:266
  293.6 12.3 %collective-permute-start.32 = (bf16[320,768]{1,0:T(8,128)(2,1)}, bf16[320,768]{1,0:T(8,128)(2,1)S(1)}, u32[]{:S(2)}, u32[]{:S(2)}) collective-permute-start(bf16[320,768]{1,0:T(8,128)(2,1)} %get-tuple-element.137), channel_id=1, source_target_pairs={{0,96},{32,0},{64,32},{96,64},{1,97},{33,1},{65,33},{97,65},{2,98}... | collective-permute-start | bytes 1474568 | tf_op jit(solution)/shard_map/ppermute | solution.py:266
  296.3 14.9 %collective-permute-start.34 = (bf16[96,2560]{1,0:T(8,128)(2,1)}, bf16[96,2560]{1,0:T(8,128)(2,1)}, u32[]{:S(2)}, u32[]{:S(2)}) collective-permute-start(bf16[96,2560]{1,0:T(8,128)(2,1)} %add_convert_fusion.7), channel_id=1, source_target_pairs={{0,0},{8,1},{16,8},{24,9},{32,16},{40,17},{48,24},{56,25},{1,32},{... | collective-permute-start | bytes 1474568 | tf_op jit(solution)/shard_map/ppermute | solution.py:477
  312.9 12.9 %copy-start.17 = (f32[1,96,2560]{2,1,0:T(8,128)S(1)}, f32[1,96,2560]{2,1,0:T(8,128)}, u32[]{:S(2)}) copy-start(f32[1,96,2560]{2,1,0:T(8,128)} %param.19) | copy-start | bytes 2949124
  312.9 12.9 %copy-start.25 = (f32[1,96,2560]{2,1,0:T(8,128)S(1)}, f32[1,96,2560]{2,1,0:T(8,128)}, u32[]{:S(2)}) copy-start(f32[1,96,2560]{2,1,0:T(8,128)} %param.22) | copy-start | bytes 2949124
  312.9 12.9 %copy-start.26 = (f32[1,96,2560]{2,1,0:T(8,128)S(1)}, f32[1,96,2560]{2,1,0:T(8,128)}, u32[]{:S(2)}) copy-start(f32[1,96,2560]{2,1,0:T(8,128)} %param.25) | copy-start | bytes 2949124
  315.0 13.9 %collective-permute-start.36 = (bf16[160,768]{1,0:T(8,128)(2,1)S(1)}, bf16[160,768]{1,0:T(8,128)(2,1)S(1)}, u32[]{:S(2)}, u32[]{:S(2)}) collective-permute-start(bf16[160,768]{1,0:T(8,128)(2,1)S(1)} %get-tuple-element.196), channel_id=1, source_target_pairs={{0,0},{8,1},{1,8},{9,9},{2,2},{10,3},{3,10},{11,11},{4,4},{12,5},{... | collective-permute-start | bytes 737288 | tf_op jit(solution)/shard_map/ppermute | solution.py:457
  322.8 7.3 %collective-permute-start.37 = (bf16[160,768]{1,0:T(8,128)(2,1)S(1)}, bf16[160,768]{1,0:T(8,128)(2,1)S(1)}, u32[]{:S(2)}, u32[]{:S(2)}) collective-permute-start(bf16[160,768]{1,0:T(8,128)(2,1)S(1)} %get-tuple-element.195), channel_id=1, source_target_pairs={{1,0},{9,1},{0,8},{8,9},{3,2},{11,3},{2,10},{10,11},{5,4},{13,5},{... | collective-permute-start | bytes 737288 | tf_op jit(solution)/shard_map/ppermute | solution.py:457
  322.9 17.0 %collective-permute-start.35 = (bf16[320,768]{1,0:T(8,128)(2,1)S(1)}, bf16[320,768]{1,0:T(8,128)(2,1)S(1)}, u32[]{:S(2)}, u32[]{:S(2)}) collective-permute-start(bf16[320,768]{1,0:T(8,128)(2,1)S(1)} %add_convert_fusion.4), channel_id=1, source_target_pairs={{0,16},{16,0},{1,17},{17,1},{2,18},{18,2},{3,19},{19,3},{4,20},{20... | collective-permute-start | bytes 1474568 | tf_op jit(solution)/shard_map/ppermute | solution.py:480
  341.9 10.8 %collective-permute-start.38 = (bf16[160,768]{1,0:T(8,128)(2,1)S(1)}, bf16[160,768]{1,0:T(8,128)(2,1)S(1)}, u32[]{:S(2)}, u32[]{:S(2)}) collective-permute-start(bf16[160,768]{1,0:T(8,128)(2,1)S(1)} %get-tuple-element.194), channel_id=1, source_target_pairs={{0,0},{8,1},{1,8},{9,9},{2,2},{10,3},{3,10},{11,11},{4,4},{12,5},{... | collective-permute-start | bytes 737288 | tf_op jit(solution)/shard_map/ppermute | solution.py:457
  347.5 6.5 %collective-permute-start.39 = (bf16[160,768]{1,0:T(8,128)(2,1)S(1)}, bf16[160,768]{1,0:T(8,128)(2,1)S(1)}, u32[]{:S(2)}, u32[]{:S(2)}) collective-permute-start(bf16[160,768]{1,0:T(8,128)(2,1)S(1)} %get-tuple-element.193), channel_id=1, source_target_pairs={{1,0},{9,1},{0,8},{8,9},{3,2},{11,3},{2,10},{10,11},{5,4},{13,5},{... | collective-permute-start | bytes 737288 | tf_op jit(solution)/shard_map/ppermute | solution.py:457
  (28 other events, 114.5 us)
where the time goes:
time: 358 us; the launch traced here: 356 us
  waiting for transfers between devices  132 us (37%)
  starting transfers between devices  87 us (24%)
  other arithmetic  44 us (12%)
  local copies, waits for them, and re-layouts  40.6 us (11%)
  Pallas kernels  29.8 us (8%)
  matrix products  21.4 us (6%)
    ppermute x6, waiting for transfers between devices, neighbours(): return (lax.ppermute(part, 'x', PLUS), lax.ppermute(part, 'x', MINUS))  33.7 us
    ppermute x6, waiting for transfers between devices, send(): lax.ppermute(to_right, 'x', PLUS)  32.3 us
    unnamed x68, local copies, waits for them, and re-layouts  23.1 us
    convert_element_type x9, other arithmetic, plus(): return sum((v.astype(f32) for v in values)).astype(bf16)  21 us
    ppermute x6, starting transfers between devices, send(): lax.ppermute(to_left, 'x', MINUS)  15.5 us
    ppermute x4, starting transfers between devices, send_home(): lax.ppermute(lax.dynamic_slice(grad, (depth * start, 0), (depth, half)),...  13.6 us
    ppermute x3, waiting for transfers between devices, far(): lax.ppermute(left[:half], 'x', PLUS)  12.8 us
    ppermute x2, waiting for transfers between devices, third(): return lax.ppermute(self.mine(1 - self.yh), 'yh', SWAP)  9.86 us
  transfers between devices with their start and end apart: 42, of which 21 were waited for; matrix products, arithmetic and copies ran while one was open for 16% of the time, Pallas kernels for 8%

commit v1 on v0

--- a/solution.py
+++ b/solution.py
@@ -478,13 +478,15 @@
     up_sum.got, gate_sent, down_home = join((up_got, gate_sent, down_home))
     up_mine, gate_sent = join((up_sum.mine(1 - yh), gate_sent))
     up_sent = lax.ppermute(up_mine, "yh", SWAP)
-    up_sum.kept = up_sum.mine(yh)
-    gate_home = send_home(gate_sum.last(gate_sent))
+    up_sum.kept, gate_sent = join((up_sum.mine(yh), gate_sent))
     new_down_weight, new_down_moment, new_down_second = adamw(
         down_weight, down_moment, down_second, down_home.astype(f32)[None]
     )
-    up_sent, gate_home = join((up_sent, gate_home))
-    up_home = send_home(up_sum.last(up_sent))
+    gate_last, new_down_weight = join((gate_sum.last(gate_sent), new_down_weight))
+    gate_home = send_home(gate_last)
+    up_last = up_sum.last(up_sent)
+    up_last, gate_home = join((up_last, gate_home))
+    up_home = send_home(up_last)
     input_grad, prob_grad = unpack_rows(ids, returned, width, capacity)
     new_gate_weight, new_gate_moment, new_gate_second = adamw(
         gate_weight, gate_moment, gate_second, natural(gate_home)

time: 358 us -> 353 us (0.986)
  waiting for transfers between devices: 132 us -> 128 us
    ppermute x4, starting transfers between devices: 13.6 us -> 7.88 us  [send_home(): lax.ppermute(lax.dynamic_slice(grad, (depth * start, 0), (depth, half)),...]
    ppermute x1, starting transfers between devices: 2.85 us -> 8.49 us  [body(): up_sent = lax.ppermute(up_mine, 'yh', SWAP)]
    ppermute x1, waiting for transfers between devices: 9.71 us -> 4.62 us  [body(): up_sent = lax.ppermute(up_mine, 'yh', SWAP)]
where the time goes in v1:
time: 353 us; the launch traced here: 351 us
  waiting for transfers between devices  128 us (36%)
  starting transfers between devices  86.9 us (25%)
  local copies, waits for them, and re-layouts  42.4 us (12%)
  other arithmetic  41 us (12%)
  Pallas kernels  29.9 us (8%)
  matrix products  21.4 us (6%)
    ppermute x6, waiting for transfers between devices, neighbours(): return (lax.ppermute(part, 'x', PLUS), lax.ppermute(part, 'x', MINUS))  33.7 us
    ppermute x6, waiting for transfers between devices, send(): lax.ppermute(to_right, 'x', PLUS)  31 us
    unnamed x68, local copies, waits for them, and re-layouts  25 us
    convert_element_type x9, other arithmetic, plus(): return sum((v.astype(f32) for v in values)).astype(bf16)  19.6 us
    ppermute x6, starting transfers between devices, send(): lax.ppermute(to_left, 'x', MINUS)  15.5 us
    ppermute x3, waiting for transfers between devices, far(): lax.ppermute(left[:half], 'x', PLUS)  12.8 us
    ppermute x2, waiting for transfers between devices, third(): return lax.ppermute(self.mine(1 - self.yh), 'yh', SWAP)  9.87 us
    pallas_call x2, Pallas kernels, input_rows(): pl.pallas_call(row_kernel, out_shape=jax.ShapeDtypeStruct((count, width),...  9 us
  transfers between devices with their start and end apart: 42, of which 21 were waited for; matrix products, arithmetic and copies ran while one was open for 16% of the time, Pallas kernels for 8%

profile of v1, /device:TPU:1, one launch (start us, length us, event | category | flops | bytes accessed | tf_op | source)
XLA Modules:
  0.0 351.4 jit_solution(9343022984362196956)
XLA Ops:
  3.5 4.6 %collective-permute-start = (bf16[160,1536]{1,0:T(8,128)(2,1)S(1)}, bf16[160,1536]{1,0:T(8,128)(2,1)S(1)}, u32[]{:S(2)}, u32[]{:S(2)}) collective-permute-start(bf16[160,1536]{1,0:T(8,128)(2,1)S(1)} %get-tuple-element.198), channel_id=1, source_target_pairs={{0,0},{1,8},{8,1},{9,9},{2,2},{3,10},{10,3},{11,11},{4,4},{5,12},{... | collective-permute-start | bytes 1474568 | tf_op jit(solution)/shard_map/ppermute | solution.py:343
  10.3 7.6 %collective-permute-done = bf16[160,1536]{1,0:T(8,128)(2,1)S(1)} collective-permute-done((bf16[160,1536]{1,0:T(8,128)(2,1)S(1)}, bf16[160,1536]{1,0:T(8,128)(2,1)S(1)}, u32[]{:S(2)}, u32[]{:S(2)}) %collective-permute-start) | collective-permute-done | bytes 491552 | tf_op jit(solution)/shard_map/ppermute | solution.py:343
  17.9 6.6 %collective-permute-done.1 = bf16[160,1536]{1,0:T(8,128)(2,1)S(1)} collective-permute-done((bf16[160,1536]{1,0:T(8,128)(2,1)S(1)}, bf16[160,1536]{1,0:T(8,128)(2,1)S(1)}, u32[]{:S(2)}, u32[]{:S(2)}) %collective-permute-start.1) | collective-permute-done | bytes 491552 | tf_op jit(solution)/shard_map/ppermute | solution.py:344
  24.4 5.3 %collective-permute-done.2 = bf16[96,2560]{1,0:T(8,128)(2,1)} collective-permute-done((bf16[96,2560]{1,0:T(8,128)(2,1)S(1)}, bf16[96,2560]{1,0:T(8,128)(2,1)}, u32[]{:S(2)}, u32[]{:S(2)}) %collective-permute-start.2) | collective-permute-done | bytes 491552 | tf_op jit(solution)/shard_map/ppermute | solution.py:345
  33.6 2.7 collective-permute-start.3
  36.6 18.1 %collective-permute-done.5.refs_2_ = bf16[320,1536]{1,0:T(8,128)(2,1)S(1)} collective-permute-done((bf16[320,1536]{1,0:T(8,128)(2,1)S(1)}, bf16[320,1536]{1,0:T(8,128)(2,1)S(1)}, u32[]{:S(2)}, u32[]{:S(2)}) %collective-permute-start.5) | collective-permute-done | bytes 983072 | tf_op jit(solution)/shard_map/ppermute | solution.py:253
  55.6 2.7 collective-permute-start.8
  64.5 3.3 collective-permute-done.4
  69.6 5.3 %all-to-all-start = ((bf16[8,48,5248]{2,1,0:T(8,128)(2,1)}), bf16[8,48,5248]{2,1,0:T(8,128)(2,1)}, u32[]{:S(2)}, u32[]{:S(2)}) async-start(bf16[8,48,5248]{2,1,0:T(8,128)(2,1)} %bitcast.57), calls=%async_computation | async-start | bytes 8060928 | tf_op jit(solution)/shard_map/all_to_all | solution.py:381
  80.7 3.1 copy-done
  85.3 11.7 %collective-permute-done.10.refs_3_ = bf16[320,1536]{1,0:T(8,128)(2,1)} collective-permute-done((bf16[320,1536]{1,0:T(8,128)(2,1)}, bf16[320,1536]{1,0:T(8,128)(2,1)}, u32[]{:S(2)}, u32[]{:S(2)}) %collective-permute-start.10) | collective-permute-done | bytes 983072 | tf_op jit(solution)/shard_map/ppermute | solution.py:253
  97.0 3.1 collective-permute-done.9.refs_2_
  100.1 2.7 collective-permute-start.12
  106.5 2.7 collective-permute-start.14
  109.3 3.2 copy-done.1
  116.2 3.1 copy-done.2
  119.3 12.8 %collective-permute-done.13.refs_1_ = bf16[160,1536]{1,0:T(8,128)(2,1)S(1)} collective-permute-done((bf16[160,1536]{1,0:T(8,128)(2,1)}, bf16[160,1536]{1,0:T(8,128)(2,1)S(1)}, u32[]{:S(2)}, u32[]{:S(2)}) %collective-permute-start.13) | collective-permute-done | bytes 491552 | tf_op jit(solution)/shard_map/ppermute | solution.py:257
  132.2 4.0 %collective-permute-start.15 = (bf16[384,5248]{1,0:T(8,128)(2,1)}, bf16[384,5248]{1,0:T(8,128)(2,1)}, u32[]{:S(2)}, u32[]{:S(2)}) collective-permute-start(bf16[384,5248]{1,0:T(8,128)(2,1)} %bitcast.6), channel_id=1, source_target_pairs={{0,1},{1,0},{2,3},{3,2},{4,5},{5,4},{6,7},{7,6},{8,9},{9,8},{10,11... | collective-permute-start | bytes 12091400 | tf_op jit(solution)/shard_map/ppermute | solution.py:397
  140.4 3.0 collective-permute-start.17
  145.2 5.2 %fusion.21 = (bf16[384,2560]{1,0:T(8,128)(2,1)S(1)}, bf16[384,2560]{1,0:T(8,128)(2,1)S(1)}) fusion(bf16[384,5248]{1,0:T(8,128)(2,1)} %bitcast.6), kind=kLoop, calls=%fused_computation.102 | loop fusion | bytes 7864320 | tf_op jit(solution)/shard_map/slice | solution.py:399
  154.0 8.6 %fusion.13 = f32[768,1536]{1,0:T(8,128)} fusion(bf16[2560,1536]{1,0:T(8,128)(2,1)S(1)} %put_rows.7.w_ref, bf16[384,2560]{1,0:T(8,128)(2,1)S(1)} %get-tuple-element.178, bf16[384,2560]{1,0:T(8,128)(2,1)S(1)} %get-tuple-element.176), kind=kOutput, calls=%fused_computation.101 | convolution fusion | flops 6047662080 | bytes 16515072 | tf_op jit(solution)/shard_map/dot_general | solution.py:402
  162.6 5.8 %convolution_convert_fusion = bf16[768,2560]{1,0:T(8,128)(2,1)S(1)} fusion(bf16[384,2560]{1,0:T(8,128)(2,1)S(1)} %get-tuple-element.177, bf16[384,2560]{1,0:T(8,128)(2,1)S(1)} %get-tuple-element.175, f32[768]{0:T(1024)S(1)} %convert_reduce_fusion, f32[768,1536]{1,0:T(8,128)} %fusion.13), kind=kOutput, calls=%fused_computation | convolution fusion | flops 3033858048 | bytes 12585984 | tf_op jit(solution)/shard_map/dot_general | solution.py:409
  173.8 7.0 %multiply_convert_fusion = (bf16[768,768]{1,0:T(8,128)(2,1)S(1)}, bf16[768,768]{1,0:T(8,128)(2,1)S(1)}, f32[768]{0:T(1024)S(1)}) fusion(f32[768]{0:T(1024)S(1)} %convert_reduce_fusion, f32[768,1536]{1,0:T(8,128)} %fusion.13, bf16[768,2560]{1,0:T(8,128)(2,1)S(1)} %put_rows.9, bf16[384,2560]{1,0:T(8,128)(2,1)S(1)} %copy-done.24, ...), kind=kOutput, calls=%fused_computation.6 | convolution fusion | flops 3038969088 | bytes 14948352 | tf_op jit(solution)/shard_map/dot_general | solution.py:417
  180.9 2.7 collective-permute-start.19
  183.8 7.5 %x_terms.1 = (bf16[2560,768]{1,0:T(8,128)(2,1)S(1)}, bf16[2560,768]{1,0:T(8,128)(2,1)S(1)}) custom-call(bf16[768,2560]{1,0:T(8,128)(2,1)S(1)} %pad_maximum_fusion.x_ref, bf16[768,768]{1,0:T(8,128)(2,1)S(1)} %get-tuple-element.128.gate_ref, bf16[768,768]{1,0:T(8,128)(2,1)S(1)} %get-tuple-element.129.up_ref), custom_call_target="tpu_custom_call" | custom-call | flops 1 | bytes 1 | tf_op jit(solution)/shard_map/x_terms/pallas_call | solution.py:174
  196.1 4.9 %input_rows.2 = bf16[384,2560]{1,0:T(8,128)(2,1)} custom-call(bf16[384,768]{1,0:T(8,128)(2,1)S(1)} %slice.211.gate_ref, bf16[384,768]{1,0:T(8,128)(2,1)S(1)} %slice.212.up_ref, bf16[2560,1536]{1,0:T(8,128)(2,1)S(1)} %put_rows.7.w_ref), custom_call_target="tpu_custom_call" | custom-call | flops 1 | bytes 1 | tf_op jit(solution)/shard_map/input_rows/pallas_call | solution.py:202
  202.0 3.3 collective-permute-done.18
  209.2 2.9 collective-permute-start.22
  212.0 2.7 collective-permute-start.24
  214.7 3.2 copy-done.5
  217.9 4.1 %input_rows.3 = bf16[384,2560]{1,0:T(8,128)(2,1)S(1)} custom-call(bf16[384,768]{1,0:T(8,128)(2,1)S(1)} %slice.181.gate_ref, bf16[384,768]{1,0:T(8,128)(2,1)S(1)} %slice.182.up_ref, bf16[2560,1536]{1,0:T(8,128)(2,1)S(1)} %copy-done.5), custom_call_target="tpu_custom_call" | custom-call | flops 1 | bytes 1 | tf_op jit(solution)/shard_map/input_rows/pallas_call | solution.py:202
  225.8 4.9 %all-to-all-start.1 = ((bf16[8,48,2688]{2,1,0:T(8,128)(2,1)}), bf16[8,48,2688]{2,1,0:T(8,128)(2,1)S(1)}, u32[]{:S(2)}, u32[]{:S(2)}) async-start(bf16[8,48,2688]{2,1,0:T(8,128)(2,1)} %bitcast.61), calls=%async_computation.1 | async-start | bytes 4128768 | tf_op jit(solution)/shard_map/all_to_all | solution.py:450
  234.3 10.6 %collective-permute-done.23 = bf16[96,2560]{1,0:T(8,128)(2,1)} collective-permute-done((bf16[96,2560]{1,0:T(8,128)(2,1)}, bf16[96,2560]{1,0:T(8,128)(2,1)}, u32[]{:S(2)}, u32[]{:S(2)}) %collective-permute-start.23) | collective-permute-done | bytes 491552 | tf_op jit(solution)/shard_map/ppermute | solution.py:266
  244.9 2.7 add_convert_fusion.12
  252.6 3.5 collective-permute-start.29
  256.2 2.7 collective-permute-start.28
  258.8 8.4 %collective-permute-done.29 = bf16[96,2560]{1,0:T(8,128)(2,1)} collective-permute-done((bf16[96,2560]{1,0:T(8,128)(2,1)}, bf16[96,2560]{1,0:T(8,128)(2,1)}, u32[]{:S(2)}, u32[]{:S(2)}) %collective-permute-start.29) | collective-permute-done | bytes 491552 | tf_op jit(solution)/shard_map/ppermute | solution.py:300
  267.2 15.0 %collective-permute-done.27 = bf16[320,768]{1,0:T(8,128)(2,1)} collective-permute-done((bf16[320,768]{1,0:T(8,128)(2,1)}, bf16[320,768]{1,0:T(8,128)(2,1)}, u32[]{:S(2)}, u32[]{:S(2)}) %collective-permute-start.27) | collective-permute-done | bytes 491552 | tf_op jit(solution)/shard_map/ppermute | solution.py:266
  282.2 2.7 add_convert_fusion.7
  290.1 3.5 collective-permute-start.33
  293.6 2.7 collective-permute-start.32
  296.3 3.7 %collective-permute-start.34 = (bf16[96,2560]{1,0:T(8,128)(2,1)}, bf16[96,2560]{1,0:T(8,128)(2,1)S(1)}, u32[]{:S(2)}, u32[]{:S(2)}) collective-permute-start(bf16[96,2560]{1,0:T(8,128)(2,1)} %add_convert_fusion.7), channel_id=1, source_target_pairs={{0,0},{8,1},{16,8},{24,9},{32,16},{40,17},{48,24},{56,25},{1,32},{... | collective-permute-start | bytes 1474568 | tf_op jit(solution)/shard_map/ppermute | solution.py:477
  305.9 5.2 %collective-permute-done.34 = bf16[96,2560]{1,0:T(8,128)(2,1)S(1)} collective-permute-done((bf16[96,2560]{1,0:T(8,128)(2,1)}, bf16[96,2560]{1,0:T(8,128)(2,1)S(1)}, u32[]{:S(2)}, u32[]{:S(2)}) %collective-permute-start.34) | collective-permute-done | bytes 491552 | tf_op jit(solution)/shard_map/ppermute | solution.py:477
  313.2 8.5 %collective-permute-start.35 = (bf16[320,768]{1,0:T(8,128)(2,1)S(1)}, bf16[320,768]{1,0:T(8,128)(2,1)S(1)}, u32[]{:S(2)}, u32[]{:S(2)}) collective-permute-start(bf16[320,768]{1,0:T(8,128)(2,1)S(1)} %get-tuple-element.150), channel_id=1, source_target_pairs={{0,16},{16,0},{1,17},{17,1},{2,18},{18,2},{3,19},{19,3},{4,20},{20... | collective-permute-start | bytes 1474568 | tf_op jit(solution)/shard_map/ppermute | solution.py:480
  328.3 4.6 %collective-permute-done.35 = bf16[320,768]{1,0:T(8,128)(2,1)S(1)} collective-permute-done((bf16[320,768]{1,0:T(8,128)(2,1)S(1)}, bf16[320,768]{1,0:T(8,128)(2,1)S(1)}, u32[]{:S(2)}, u32[]{:S(2)}) %collective-permute-start.35) | collective-permute-done | bytes 491552 | tf_op jit(solution)/shard_map/ppermute | solution.py:480
  333.1 4.1 %collective-permute-done.36 = bf16[160,768]{1,0:T(8,128)(2,1)S(1)} collective-permute-done((bf16[160,768]{1,0:T(8,128)(2,1)S(1)}, bf16[160,768]{1,0:T(8,128)(2,1)S(1)}, u32[]{:S(2)}, u32[]{:S(2)}) %collective-permute-start.36) | collective-permute-done | bytes 245792 | tf_op jit(solution)/shard_map/ppermute | solution.py:457
  337.3 5.3 %collective-permute-start.38 = (bf16[160,768]{1,0:T(8,128)(2,1)S(1)}, bf16[160,768]{1,0:T(8,128)(2,1)S(1)}, u32[]{:S(2)}, u32[]{:S(2)}) collective-permute-start(bf16[160,768]{1,0:T(8,128)(2,1)S(1)} %get-tuple-element.204), channel_id=1, source_target_pairs={{0,0},{8,1},{1,8},{9,9},{2,2},{10,3},{3,10},{11,11},{4,4},{12,5},{... | collective-permute-start | bytes 737288 | tf_op jit(solution)/shard_map/ppermute | solution.py:457
  344.9 2.9 collective-permute-done.38
  (179 shorter events, 95.8 us)
Async XLA Ops:
  3.5 14.3 %collective-permute-start = (bf16[160,1536]{1,0:T(8,128)(2,1)S(1)}, bf16[160,1536]{1,0:T(8,128)(2,1)S(1)}, u32[]{:S(2)}, u32[]{:S(2)}) collective-permute-start(bf16[160,1536]{1,0:T(8,128)(2,1)S(1)} %get-tuple-element.198), channel_id=1, source_target_pairs={{0,0},{1,8},{8,1},{9,9},{2,2},{3,10},{10,3},{11,11},{4,4},{5,12},{... | collective-permute-start | bytes 1474568 | tf_op jit(solution)/shard_map/ppermute | solution.py:343
  8.2 50.1 %copy-start.33 = (bf16[128,2]{0,1:T(2,128)(2,1)S(1)}, bf16[128,2]{0,1:T(2,128)(2,1)}, u32[]{:S(2)}) copy-start(bf16[128,2]{0,1:T(2,128)(2,1)} %param.16) | copy-start | bytes 1540
  8.2 50.1 %copy-start.15 = (s32[128,2]{0,1:T(2,128)S(1)}, s32[128,2]{0,1:T(2,128)}, u32[]{:S(2)}) copy-start(s32[128,2]{0,1:T(2,128)} %param.15) | copy-start | bytes 3076
  8.2 16.3 %collective-permute-start.1 = (bf16[160,1536]{1,0:T(8,128)(2,1)S(1)}, bf16[160,1536]{1,0:T(8,128)(2,1)S(1)}, u32[]{:S(2)}, u32[]{:S(2)}) collective-permute-start(bf16[160,1536]{1,0:T(8,128)(2,1)S(1)} %get-tuple-element.197), channel_id=1, source_target_pairs={{0,1},{1,9},{8,0},{9,8},{2,3},{3,11},{10,2},{11,10},{4,5},{5,13},{... | collective-permute-start | bytes 1474568 | tf_op jit(solution)/shard_map/ppermute | solution.py:344
  8.3 21.4 %collective-permute-start.2 = (bf16[96,2560]{1,0:T(8,128)(2,1)S(1)}, bf16[96,2560]{1,0:T(8,128)(2,1)}, u32[]{:S(2)}, u32[]{:S(2)}) collective-permute-start(bf16[96,2560]{1,0:T(8,128)(2,1)S(1)} %convert_bitcast_fusion), channel_id=1, source_target_pairs={{0,0},{1,8},{8,16},{9,24},{16,32},{17,40},{24,48},{25,56},{32,1},{... | collective-permute-start | bytes 1474568 | tf_op jit(solution)/shard_map/ppermute | solution.py:345
  30.0 24.7 %collective-permute-start.5 = (bf16[320,1536]{1,0:T(8,128)(2,1)S(1)}, bf16[320,1536]{1,0:T(8,128)(2,1)S(1)}, u32[]{:S(2)}, u32[]{:S(2)}) collective-permute-start(bf16[320,1536]{1,0:T(8,128)(2,1)S(1)} %maximum_select_fusion.refs_1_), channel_id=1, source_target_pairs={{0,32},{32,64},{64,96},{96,0},{1,33},{33,65},{65,97},{97,1},{2,34}... | collective-permute-start | bytes 2949128 | tf_op jit(solution)/shard_map/ppermute | solution.py:253
  32.2 23.2 %collective-permute-start.6 = (bf16[320,1536]{1,0:T(8,128)(2,1)S(1)}, bf16[320,1536]{1,0:T(8,128)(2,1)S(1)}, u32[]{:S(2)}, u32[]{:S(2)}) collective-permute-start(bf16[320,1536]{1,0:T(8,128)(2,1)S(1)} %maximum_select_fusion.refs_1_), channel_id=1, source_target_pairs={{0,96},{32,0},{64,32},{96,64},{1,97},{33,1},{65,33},{97,65},{2,98}... | collective-permute-start | bytes 2949128 | tf_op jit(solution)/shard_map/ppermute | solution.py:253
  33.6 34.2 %collective-permute-start.3 = (bf16[320,1536]{1,0:T(8,128)(2,1)S(1)}, bf16[320,1536]{1,0:T(8,128)(2,1)S(1)}, u32[]{:S(2)}, u32[]{:S(2)}) collective-permute-start(bf16[320,1536]{1,0:T(8,128)(2,1)S(1)} %maximum_select_fusion.refs_1_), channel_id=1, source_target_pairs={{0,16},{16,0},{1,17},{17,1},{2,18},{18,2},{3,19},{19,3},{4,20},{20... | collective-permute-start | bytes 2949128 | tf_op jit(solution)/shard_map/ppermute | solution.py:351
  36.2 31.5 %collective-permute-start.4 = (bf16[96,2560]{1,0:T(8,128)(2,1)}, bf16[96,2560]{1,0:T(8,128)(2,1)S(1)}, u32[]{:S(2)}, u32[]{:S(2)}) collective-permute-start(bf16[96,2560]{1,0:T(8,128)(2,1)} %collective-permute-done.2), channel_id=1, source_target_pairs={{0,16},{16,0},{1,17},{17,1},{2,18},{18,2},{3,19},{19,3},{4,20},{20... | collective-permute-start | bytes 1474568 | tf_op jit(solution)/shard_map/ppermute | solution.py:352
  55.4 13.3 %collective-permute-start.7 = (bf16[160,1536]{1,0:T(8,128)(2,1)S(1)}, bf16[160,1536]{1,0:T(8,128)(2,1)S(1)}, u32[]{:S(2)}, u32[]{:S(2)}) collective-permute-start(bf16[160,1536]{1,0:T(8,128)(2,1)S(1)} %slice.157), channel_id=1, source_target_pairs={{0,32},{32,64},{64,96},{96,0},{1,33},{33,65},{65,97},{97,1},{2,34}... | collective-permute-start | bytes 1474568 | tf_op jit(solution)/shard_map/ppermute | solution.py:257
  55.6 13.2 %collective-permute-start.8 = (bf16[160,1536]{1,0:T(8,128)(2,1)S(1)}, bf16[160,1536]{1,0:T(8,128)(2,1)S(1)}, u32[]{:S(2)}, u32[]{:S(2)}) collective-permute-start(bf16[160,1536]{1,0:T(8,128)(2,1)S(1)} %slice.158), channel_id=1, source_target_pairs={{0,96},{32,0},{64,32},{96,64},{1,97},{33,1},{65,33},{97,65},{2,98}... | collective-permute-start | bytes 1474568 | tf_op jit(solution)/shard_map/ppermute | solution.py:257
  69.6 62.5 %all-to-all-start = ((bf16[8,48,5248]{2,1,0:T(8,128)(2,1)}), bf16[8,48,5248]{2,1,0:T(8,128)(2,1)}, u32[]{:S(2)}, u32[]{:S(2)}) async-start(bf16[8,48,5248]{2,1,0:T(8,128)(2,1)} %bitcast.57), calls=%async_computation | async-start | bytes 8060928 | tf_op jit(solution)/shard_map/all_to_all | solution.py:381
  74.9 22.1 %collective-permute-start.10 = (bf16[320,1536]{1,0:T(8,128)(2,1)}, bf16[320,1536]{1,0:T(8,128)(2,1)}, u32[]{:S(2)}, u32[]{:S(2)}) collective-permute-start(bf16[320,1536]{1,0:T(8,128)(2,1)} %copy-done.9), channel_id=1, source_target_pairs={{0,96},{32,0},{64,32},{96,64},{1,97},{33,1},{65,33},{97,65},{2,98}... | collective-permute-start | bytes 2949128 | tf_op jit(solution)/shard_map/ppermute | solution.py:253
  77.4 22.7 %collective-permute-start.9 = (bf16[320,1536]{1,0:T(8,128)(2,1)}, bf16[320,1536]{1,0:T(8,128)(2,1)}, u32[]{:S(2)}, u32[]{:S(2)}) collective-permute-start(bf16[320,1536]{1,0:T(8,128)(2,1)} %copy-done.9), channel_id=1, source_target_pairs={{0,32},{32,64},{64,96},{96,0},{1,33},{33,65},{65,97},{97,1},{2,34}... | collective-permute-start | bytes 2949128 | tf_op jit(solution)/shard_map/ppermute | solution.py:253
  100.1 32.0 %collective-permute-start.11 = (bf16[192,2560]{1,0:T(8,128)(2,1)S(1)}, bf16[192,2560]{1,0:T(8,128)(2,1)S(1)}, u32[]{:S(2)}, u32[]{:S(2)}) collective-permute-start(bf16[192,2560]{1,0:T(8,128)(2,1)S(1)} %maximum_select_fusion.1.refs_1_), channel_id=1, source_target_pairs={{0,32},{32,64},{64,96},{96,0},{1,33},{33,65},{65,97},{97,1},{2,34}... | collective-permute-start | bytes 2949128 | tf_op jit(solution)/shard_map/ppermute | solution.py:253
  100.1 32.0 %collective-permute-start.12 = (bf16[192,2560]{1,0:T(8,128)(2,1)S(1)}, bf16[192,2560]{1,0:T(8,128)(2,1)S(1)}, u32[]{:S(2)}, u32[]{:S(2)}) collective-permute-start(bf16[192,2560]{1,0:T(8,128)(2,1)S(1)} %maximum_select_fusion.1.refs_1_), channel_id=1, source_target_pairs={{0,96},{32,0},{64,32},{96,64},{1,97},{33,1},{65,33},{97,65},{2,98}... | collective-permute-start | bytes 2949128 | tf_op jit(solution)/shard_map/ppermute | solution.py:253
  104.7 27.5 %collective-permute-start.13 = (bf16[160,1536]{1,0:T(8,128)(2,1)}, bf16[160,1536]{1,0:T(8,128)(2,1)S(1)}, u32[]{:S(2)}, u32[]{:S(2)}) collective-permute-start(bf16[160,1536]{1,0:T(8,128)(2,1)} %slice.159), channel_id=1, source_target_pairs={{0,32},{32,64},{64,96},{96,0},{1,33},{33,65},{65,97},{97,1},{2,34}... | collective-permute-start | bytes 1474568 | tf_op jit(solution)/shard_map/ppermute | solution.py:257
  106.5 25.6 %collective-permute-start.14 = (bf16[160,1536]{1,0:T(8,128)(2,1)}, bf16[160,1536]{1,0:T(8,128)(2,1)}, u32[]{:S(2)}, u32[]{:S(2)}) collective-permute-start(bf16[160,1536]{1,0:T(8,128)(2,1)} %slice.160), channel_id=1, source_target_pairs={{0,96},{32,0},{64,32},{96,64},{1,97},{33,1},{65,33},{97,65},{2,98}... | collective-permute-start | bytes 1474568 | tf_op jit(solution)/shard_map/ppermute | solution.py:257
  132.2 18.3 %collective-permute-start.15 = (bf16[384,5248]{1,0:T(8,128)(2,1)}, bf16[384,5248]{1,0:T(8,128)(2,1)}, u32[]{:S(2)}, u32[]{:S(2)}) collective-permute-start(bf16[384,5248]{1,0:T(8,128)(2,1)} %bitcast.6), channel_id=1, source_target_pairs={{0,1},{1,0},{2,3},{3,2},{4,5},{5,4},{6,7},{7,6},{8,9},{9,8},{10,11... | collective-permute-start | bytes 12091400 | tf_op jit(solution)/shard_map/ppermute | solution.py:397
  140.3 31.4 %collective-permute-start.16 = (bf16[96,2560]{1,0:T(8,128)(2,1)}, bf16[96,2560]{1,0:T(8,128)(2,1)S(1)}, u32[]{:S(2)}, u32[]{:S(2)}) collective-permute-start(bf16[96,2560]{1,0:T(8,128)(2,1)} %slice.168), channel_id=1, source_target_pairs={{0,32},{32,64},{64,96},{96,0},{1,33},{33,65},{65,97},{97,1},{2,34}... | collective-permute-start | bytes 1474568 | tf_op jit(solution)/shard_map/ppermute | solution.py:257
  140.4 31.3 %collective-permute-start.17 = (bf16[96,2560]{1,0:T(8,128)(2,1)}, bf16[96,2560]{1,0:T(8,128)(2,1)S(1)}, u32[]{:S(2)}, u32[]{:S(2)}) collective-permute-start(bf16[96,2560]{1,0:T(8,128)(2,1)} %slice.169), channel_id=1, source_target_pairs={{0,96},{32,0},{64,32},{96,64},{1,97},{33,1},{65,33},{97,65},{2,98}... | collective-permute-start | bytes 1474568 | tf_op jit(solution)/shard_map/ppermute | solution.py:257
  145.2 50.9 %copy-start.4 = (bf16[2560,1536]{1,0:T(8,128)(2,1)}, bf16[2560,1536]{1,0:T(8,128)(2,1)S(1)}, u32[]{:S(2)}) copy-start(bf16[2560,1536]{1,0:T(8,128)(2,1)S(1)} %put_rows.7.w_ref) | copy-start | bytes 23592964
  180.8 24.5 %collective-permute-start.18 = (bf16[192,2560]{1,0:T(8,128)(2,1)}, bf16[192,2560]{1,0:T(8,128)(2,1)S(1)}, u32[]{:S(2)}, u32[]{:S(2)}) collective-permute-start(bf16[192,2560]{1,0:T(8,128)(2,1)} %pad_maximum_fusion.5), channel_id=1, source_target_pairs={{0,32},{32,64},{64,96},{96,0},{1,33},{33,65},{65,97},{97,1},{2,34}... | collective-permute-start | bytes 2949128 | tf_op jit(solution)/shard_map/ppermute | solution.py:266
  180.9 24.4 %collective-permute-start.19 = (bf16[192,2560]{1,0:T(8,128)(2,1)}, bf16[192,2560]{1,0:T(8,128)(2,1)}, u32[]{:S(2)}, u32[]{:S(2)}) collective-permute-start(bf16[192,2560]{1,0:T(8,128)(2,1)} %pad_maximum_fusion.6), channel_id=1, source_target_pairs={{0,96},{32,0},{64,32},{96,64},{1,97},{33,1},{65,33},{97,65},{2,98}... | collective-permute-start | bytes 2949128 | tf_op jit(solution)/shard_map/ppermute | solution.py:266
  193.3 8.7 %collective-permute-start.20 = (f32[384,128]{1,0:T(8,128)S(1)}, f32[384,128]{1,0:T(8,128)S(1)}, u32[]{:S(2)}, u32[]{:S(2)}) collective-permute-start(f32[384,128]{1,0:T(8,128)S(1)} %broadcast_in_dim.2), channel_id=1, source_target_pairs={{0,1},{1,0},{2,3},{3,2},{4,5},{5,4},{6,7},{7,6},{8,9},{9,8},{10,11... | collective-permute-start | bytes 589832 | tf_op jit(solution)/shard_map/ppermute | solution.py:431
  205.3 16.9 %collective-permute-start.30 = (bf16[384,2560]{1,0:T(8,128)(2,1)}, bf16[384,2560]{1,0:T(8,128)(2,1)}, u32[]{:S(2)}, u32[]{:S(2)}) collective-permute-start(bf16[384,2560]{1,0:T(8,128)(2,1)} %input_rows.2), channel_id=1, source_target_pairs={{0,1},{1,0},{2,3},{3,2},{4,5},{5,4},{6,7},{7,6},{8,9},{9,8},{10,11... | collective-permute-start | bytes 5898248 | tf_op jit(solution)/shard_map/ppermute | solution.py:439
  209.1 35.8 %collective-permute-start.21 = (bf16[640,768]{1,0:T(8,128)(2,1)}, bf16[640,768]{1,0:T(8,128)(2,1)}, u32[]{:S(2)}, u32[]{:S(2)}) collective-permute-start(bf16[640,768]{1,0:T(8,128)(2,1)} %pad_maximum_fusion.7), channel_id=1, source_target_pairs={{0,32},{32,64},{64,96},{96,0},{1,33},{33,65},{65,97},{97,1},{2,34}... | collective-permute-start | bytes 2949128 | tf_op jit(solution)/shard_map/ppermute | solution.py:266
  209.2 35.7 %collective-permute-start.22 = (bf16[640,768]{1,0:T(8,128)(2,1)}, bf16[640,768]{1,0:T(8,128)(2,1)}, u32[]{:S(2)}, u32[]{:S(2)}) collective-permute-start(bf16[640,768]{1,0:T(8,128)(2,1)} %pad_maximum_fusion.8), channel_id=1, source_target_pairs={{0,96},{32,0},{64,32},{96,64},{1,97},{33,1},{65,33},{97,65},{2,98}... | collective-permute-start | bytes 2949128 | tf_op jit(solution)/shard_map/ppermute | solution.py:266
  212.0 32.8 %collective-permute-start.23 = (bf16[96,2560]{1,0:T(8,128)(2,1)}, bf16[96,2560]{1,0:T(8,128)(2,1)}, u32[]{:S(2)}, u32[]{:S(2)}) collective-permute-start(bf16[96,2560]{1,0:T(8,128)(2,1)} %get-tuple-element.117), channel_id=1, source_target_pairs={{0,32},{32,64},{64,96},{96,0},{1,33},{33,65},{65,97},{97,1},{2,34}... | collective-permute-start | bytes 1474568 | tf_op jit(solution)/shard_map/ppermute | solution.py:266
  212.0 32.8 %collective-permute-start.24 = (bf16[96,2560]{1,0:T(8,128)(2,1)}, bf16[96,2560]{1,0:T(8,128)(2,1)}, u32[]{:S(2)}, u32[]{:S(2)}) collective-permute-start(bf16[96,2560]{1,0:T(8,128)(2,1)} %get-tuple-element.118), channel_id=1, source_target_pairs={{0,96},{32,0},{64,32},{96,64},{1,97},{33,1},{65,33},{97,65},{2,98}... | collective-permute-start | bytes 1474568 | tf_op jit(solution)/shard_map/ppermute | solution.py:266
  225.8 56.4 %all-to-all-start.1 = ((bf16[8,48,2688]{2,1,0:T(8,128)(2,1)}), bf16[8,48,2688]{2,1,0:T(8,128)(2,1)S(1)}, u32[]{:S(2)}, u32[]{:S(2)}) async-start(bf16[8,48,2688]{2,1,0:T(8,128)(2,1)} %bitcast.61), calls=%async_computation.1 | async-start | bytes 4128768 | tf_op jit(solution)/shard_map/all_to_all | solution.py:450
  247.5 34.7 %collective-permute-start.25 = (bf16[640,768]{1,0:T(8,128)(2,1)}, bf16[640,768]{1,0:T(8,128)(2,1)}, u32[]{:S(2)}, u32[]{:S(2)}) collective-permute-start(bf16[640,768]{1,0:T(8,128)(2,1)} %pad_maximum_fusion.9), channel_id=1, source_target_pairs={{0,32},{32,64},{64,96},{96,0},{1,33},{33,65},{65,97},{97,1},{2,34}... | collective-permute-start | bytes 2949128 | tf_op jit(solution)/shard_map/ppermute | solution.py:266
  248.2 34.0 %collective-permute-start.26 = (bf16[640,768]{1,0:T(8,128)(2,1)}, bf16[640,768]{1,0:T(8,128)(2,1)}, u32[]{:S(2)}, u32[]{:S(2)}) collective-permute-start(bf16[640,768]{1,0:T(8,128)(2,1)} %pad_maximum_fusion.10), channel_id=1, source_target_pairs={{0,96},{32,0},{64,32},{96,64},{1,97},{33,1},{65,33},{97,65},{2,98}... | collective-permute-start | bytes 2949128 | tf_op jit(solution)/shard_map/ppermute | solution.py:266
  252.6 14.5 %collective-permute-start.29 = (bf16[96,2560]{1,0:T(8,128)(2,1)}, bf16[96,2560]{1,0:T(8,128)(2,1)}, u32[]{:S(2)}, u32[]{:S(2)}) collective-permute-start(bf16[96,2560]{1,0:T(8,128)(2,1)} %add_convert_fusion.11), channel_id=1, source_target_pairs={{0,16},{16,0},{1,17},{17,1},{2,18},{18,2},{3,19},{19,3},{4,20},{20... | collective-permute-start | bytes 1474568 | tf_op jit(solution)/shard_map/ppermute | solution.py:300
  256.2 26.1 %collective-permute-start.27 = (bf16[320,768]{1,0:T(8,128)(2,1)}, bf16[320,768]{1,0:T(8,128)(2,1)}, u32[]{:S(2)}, u32[]{:S(2)}) collective-permute-start(bf16[320,768]{1,0:T(8,128)(2,1)} %get-tuple-element.124), channel_id=1, source_target_pairs={{0,32},{32,64},{64,96},{96,0},{1,33},{33,65},{65,97},{97,1},{2,34}... | collective-permute-start | bytes 1474568 | tf_op jit(solution)/shard_map/ppermute | solution.py:266
  256.2 26.1 %collective-permute-start.28 = (bf16[320,768]{1,0:T(8,128)(2,1)}, bf16[320,768]{1,0:T(8,128)(2,1)}, u32[]{:S(2)}, u32[]{:S(2)}) collective-permute-start(bf16[320,768]{1,0:T(8,128)(2,1)} %get-tuple-element.125), channel_id=1, source_target_pairs={{0,96},{32,0},{64,32},{96,64},{1,97},{33,1},{65,33},{97,65},{2,98}... | collective-permute-start | bytes 1474568 | tf_op jit(solution)/shard_map/ppermute | solution.py:266
  290.1 13.7 %collective-permute-start.33 = (bf16[320,768]{1,0:T(8,128)(2,1)}, bf16[320,768]{1,0:T(8,128)(2,1)S(1)}, u32[]{:S(2)}, u32[]{:S(2)}) collective-permute-start(bf16[320,768]{1,0:T(8,128)(2,1)} %add_convert_fusion.6), channel_id=1, source_target_pairs={{0,16},{16,0},{1,17},{17,1},{2,18},{18,2},{3,19},{19,3},{4,20},{20... | collective-permute-start | bytes 1474568 | tf_op jit(solution)/shard_map/ppermute | solution.py:300
  293.6 12.3 %collective-permute-start.31 = (bf16[320,768]{1,0:T(8,128)(2,1)}, bf16[320,768]{1,0:T(8,128)(2,1)S(1)}, u32[]{:S(2)}, u32[]{:S(2)}) collective-permute-start(bf16[320,768]{1,0:T(8,128)(2,1)} %get-tuple-element.140), channel_id=1, source_target_pairs={{0,32},{32,64},{64,96},{96,0},{1,33},{33,65},{65,97},{97,1},{2,34}... | collective-permute-start | bytes 1474568 | tf_op jit(solution)/shard_map/ppermute | solution.py:266
  293.6 12.3 %collective-permute-start.32 = (bf16[320,768]{1,0:T(8,128)(2,1)}, bf16[320,768]{1,0:T(8,128)(2,1)}, u32[]{:S(2)}, u32[]{:S(2)}) collective-permute-start(bf16[320,768]{1,0:T(8,128)(2,1)} %get-tuple-element.141), channel_id=1, source_target_pairs={{0,96},{32,0},{64,32},{96,64},{1,97},{33,1},{65,33},{97,65},{2,98}... | collective-permute-start | bytes 1474568 | tf_op jit(solution)/shard_map/ppermute | solution.py:266
  296.3 14.9 %collective-permute-start.34 = (bf16[96,2560]{1,0:T(8,128)(2,1)}, bf16[96,2560]{1,0:T(8,128)(2,1)S(1)}, u32[]{:S(2)}, u32[]{:S(2)}) collective-permute-start(bf16[96,2560]{1,0:T(8,128)(2,1)} %add_convert_fusion.7), channel_id=1, source_target_pairs={{0,0},{8,1},{16,8},{24,9},{32,16},{40,17},{48,24},{56,25},{1,32},{... | collective-permute-start | bytes 1474568 | tf_op jit(solution)/shard_map/ppermute | solution.py:477
  302.3 19.4 %copy-start.17 = (f32[1,96,2560]{2,1,0:T(8,128)S(1)}, f32[1,96,2560]{2,1,0:T(8,128)}, u32[]{:S(2)}) copy-start(f32[1,96,2560]{2,1,0:T(8,128)} %param.19) | copy-start | bytes 2949124
  302.3 19.4 %copy-start.25 = (f32[1,96,2560]{2,1,0:T(8,128)S(1)}, f32[1,96,2560]{2,1,0:T(8,128)}, u32[]{:S(2)}) copy-start(f32[1,96,2560]{2,1,0:T(8,128)} %param.22) | copy-start | bytes 2949124
  302.3 19.4 %copy-start.26 = (f32[1,96,2560]{2,1,0:T(8,128)S(1)}, f32[1,96,2560]{2,1,0:T(8,128)}, u32[]{:S(2)}) copy-start(f32[1,96,2560]{2,1,0:T(8,128)} %param.25) | copy-start | bytes 2949124
  313.2 19.7 %collective-permute-start.35 = (bf16[320,768]{1,0:T(8,128)(2,1)S(1)}, bf16[320,768]{1,0:T(8,128)(2,1)S(1)}, u32[]{:S(2)}, u32[]{:S(2)}) collective-permute-start(bf16[320,768]{1,0:T(8,128)(2,1)S(1)} %get-tuple-element.150), channel_id=1, source_target_pairs={{0,16},{16,0},{1,17},{17,1},{2,18},{18,2},{3,19},{19,3},{4,20},{20... | collective-permute-start | bytes 1474568 | tf_op jit(solution)/shard_map/ppermute | solution.py:480
  325.8 11.4 %collective-permute-start.36 = (bf16[160,768]{1,0:T(8,128)(2,1)S(1)}, bf16[160,768]{1,0:T(8,128)(2,1)S(1)}, u32[]{:S(2)}, u32[]{:S(2)}) collective-permute-start(bf16[160,768]{1,0:T(8,128)(2,1)S(1)} %get-tuple-element.206), channel_id=1, source_target_pairs={{0,0},{8,1},{1,8},{9,9},{2,2},{10,3},{3,10},{11,11},{4,4},{12,5},{... | collective-permute-start | bytes 737288 | tf_op jit(solution)/shard_map/ppermute | solution.py:457
  328.0 9.2 %collective-permute-start.37 = (bf16[160,768]{1,0:T(8,128)(2,1)S(1)}, bf16[160,768]{1,0:T(8,128)(2,1)S(1)}, u32[]{:S(2)}, u32[]{:S(2)}) collective-permute-start(bf16[160,768]{1,0:T(8,128)(2,1)S(1)} %get-tuple-element.205), channel_id=1, source_target_pairs={{1,0},{9,1},{0,8},{8,9},{3,2},{11,3},{2,10},{10,11},{5,4},{13,5},{... | collective-permute-start | bytes 737288 | tf_op jit(solution)/shard_map/ppermute | solution.py:457
  337.3 10.5 %collective-permute-start.38 = (bf16[160,768]{1,0:T(8,128)(2,1)S(1)}, bf16[160,768]{1,0:T(8,128)(2,1)S(1)}, u32[]{:S(2)}, u32[]{:S(2)}) collective-permute-start(bf16[160,768]{1,0:T(8,128)(2,1)S(1)} %get-tuple-element.204), channel_id=1, source_target_pairs={{0,0},{8,1},{1,8},{9,9},{2,2},{10,3},{3,10},{11,11},{4,4},{12,5},{... | collective-permute-start | bytes 737288 | tf_op jit(solution)/shard_map/ppermute | solution.py:457
  342.6 6.5 %collective-permute-start.39 = (bf16[160,768]{1,0:T(8,128)(2,1)S(1)}, bf16[160,768]{1,0:T(8,128)(2,1)S(1)}, u32[]{:S(2)}, u32[]{:S(2)}) collective-permute-start(bf16[160,768]{1,0:T(8,128)(2,1)S(1)} %get-tuple-element.203), channel_id=1, source_target_pairs={{1,0},{9,1},{0,8},{8,9},{3,2},{11,3},{2,10},{10,11},{5,4},{13,5},{... | collective-permute-start | bytes 737288 | tf_op jit(solution)/shard_map/ppermute | solution.py:457
  (28 other events, 135.6 us)
